TPU v7x, 256 devices: a whole 4x4x8 slice. The times are simulated.
256 devices in a mesh: group: 8 (over x, core), inner: 32 (over z, y).
Axes of the slice: x: 4, y: 4, z: 8, core: 2. Of those that a mesh axis runs over, the one named last changes fastest.
Arguments:
- x_self: bfloat16 [262144, 256], P(('group', 'inner')), may hold values from -6 to 6
- x_agg: bfloat16 [262144, 256], P(('group', 'inner')), may hold values from -6 to 6
- w_self: bfloat16 [256, 256], replicated, may hold values from -0.25 to 0.25
- w_nbr: bfloat16 [256, 256], replicated, may hold values from -0.25 to 0.25
- b_layer: float32 [256], replicated, may hold values from -3 to 3
- w_one: bfloat16 [256, 512], replicated, may hold values from -0.375 to 0.375
- b_one: float32 [512], replicated, may hold values from -3 to 3
- w_two: bfloat16 [512, 512], replicated, may hold values from -0.25 to 0.25
- b_two: float32 [512], replicated, may hold values from -3 to 3
- w_out: float32 [512], replicated, may hold values from -2 to 2
- send_lists: int32 [2048, 32, 12], P(('group', 'inner')), may hold values from 0 to 1023, as said below
- endpoint_slots: int32 [131072, 2], P(('group', 'inner')), may hold values from 0 to 3071, as said below
- neg_index: int32 [131072, 4], P(('group', 'inner')), may hold values from 0 to 511, as said below
Outputs:
- grad_self: bfloat16 [262144, 256], P(('group', 'inner'))
- grad_agg: bfloat16 [262144, 256], P(('group', 'inner'))
- grad_scorer: float32 [393216], P(('group', 'inner'))
- grad_layer: float32 [131072], P(('group', 'inner'))
- grad_bias: float32 [1792], replicated
Inputs may be any that keep to these rules, and one draw needn't show every extreme that they name: `send_lists`: viewed as [256, 256, 12] (owner, requesting device, slot), each entry is a row of the owner's block of 1024 nodes, and the 12 entries of one owner and one requesting device are distinct. Slots that endpoint_slots never names hold arbitrary rows. `endpoint_slots`: each entry of device r's block is a slot o * 12 + c of that device and names the node of send_lists' entry (o, r, c). `neg_index`: entry [p, k] is the index, within the same block of 512 positives, of another positive whose destination serves as the k-th negative of p; it is never p itself.
All inputs are finite; a program needn't handle non-finite values.
Results may differ from a plain program's by a relative error of at most 0.0075.
Values may be sent and summed in bfloat16 or wider, within the bound.
No kernel may reach another device: no remote copies, remote signals or barrier semaphores. Data moves between devices by JAX's collectives and lax.ppermute only.
A program may use at most 128 MiB of HBM per device.

v0:
```python
import jax
import jax.numpy as jnp
from jax import lax
from jax.sharding import PartitionSpec as P


def silu_slope(inputs):
    sigmoid_of = jax.nn.sigmoid(inputs)
    return sigmoid_of * (1.0 + inputs * (1.0 - sigmoid_of))


def dot_first(first_op, second_op):
    return lax.dot_general(
        first_op, second_op, (((0,), (0,)), ((), ())), preferred_element_type=jnp.float32
    )


def dot_last(first_op, second_op):
    return lax.dot_general(
        first_op, second_op, (((1,), (1,)), ((), ())), preferred_element_type=jnp.float32
    )


def body(
    x_self,
    x_agg,
    w_self,
    w_nbr,
    b_layer,
    w_one,
    b_one,
    w_two,
    b_two,
    w_out,
    send_lists,
    endpoint_slots,
    neg_index,
):
    groups = lax.axis_size("group")
    inners = lax.axis_size("inner")
    owners = groups * inners
    feature_width = x_self.shape[1]
    pos_rows = endpoint_slots.shape[0]
    negatives = neg_index.shape[1]
    capacity = send_lists.shape[2]
    pairs_dev = pos_rows * (1 + negatives)
    pre_act = (
        jnp.dot(x_self, w_self, preferred_element_type=jnp.float32)
        + jnp.dot(x_agg, w_nbr, preferred_element_type=jnp.float32)
        + b_layer
    )
    node_table = jax.nn.silu(pre_act).astype(jnp.bfloat16)
    flat_lists = send_lists.reshape(-1)
    outgoing = jnp.take(node_table, flat_lists, axis=0).reshape(
        groups, inners, capacity, feature_width
    )
    fetched = lax.all_to_all(
        lax.all_to_all(outgoing, "group", split_axis=0, concat_axis=0, tiled=True),
        "inner",
        split_axis=1,
        concat_axis=1,
        tiled=True,
    )
    slot_rows = fetched.reshape(owners * capacity, feature_width)
    src_rows = jnp.take(slot_rows, endpoint_slots[:, 0], axis=0)
    dst_rows = jnp.take(slot_rows, endpoint_slots[:, 1], axis=0)
    neg_flat = neg_index.T.reshape(-1)
    right_rows = jnp.concatenate([dst_rows, jnp.take(dst_rows, neg_flat, axis=0)], axis=0)
    left_rows = jnp.tile(src_rows, (1 + negatives, 1))
    labels = (jnp.arange(pairs_dev, dtype=jnp.int32) < pos_rows).astype(jnp.float32)
    joint_rows = (left_rows.astype(jnp.float32) * right_rows.astype(jnp.float32)).astype(
        jnp.bfloat16
    )
    a_one = jnp.dot(joint_rows, w_one, preferred_element_type=jnp.float32) + b_one
    h_one = jax.nn.silu(a_one).astype(jnp.bfloat16)
    a_two = jnp.dot(h_one, w_two, preferred_element_type=jnp.float32) + b_two
    h_two = jax.nn.silu(a_two)
    scores = jnp.sum(h_two * w_out, axis=1)
    loss_slope = jax.nn.sigmoid(scores) - labels
    d_two = loss_slope[:, None] * w_out * silu_slope(a_two)
    d_two_low = d_two.astype(jnp.bfloat16)
    d_one = dot_last(d_two_low, w_two) * silu_slope(a_one)
    d_one_low = d_one.astype(jnp.bfloat16)
    d_joint = dot_last(d_one_low, w_one)
    scorer_term = (
        jnp.concatenate(
            [dot_first(joint_rows, d_one_low).reshape(-1), dot_first(h_one, d_two_low).reshape(-1)]
        )
        / pairs_dev
    )
    scorer_share = None
    d_left = d_joint * right_rows
    d_right = d_joint * left_rows
    grad_src = jnp.sum(d_left.reshape(1 + negatives, pos_rows, feature_width), axis=0)
    grad_dst = d_right[:pos_rows] + jax.ops.segment_sum(
        d_right[pos_rows:], neg_flat, num_segments=pos_rows
    )
    slot_grads = jax.ops.segment_sum(
        jnp.concatenate([grad_src, grad_dst], axis=0),
        endpoint_slots.T.reshape(-1),
        num_segments=owners * capacity,
    )
    outbound = slot_grads.reshape(groups, inners, capacity, feature_width)
    received = lax.all_to_all(
        lax.all_to_all(outbound, "group", split_axis=0, concat_axis=0, tiled=True),
        "inner",
        split_axis=1,
        concat_axis=1,
        tiled=True,
    )
    node_grads = jax.ops.segment_sum(
        received.reshape(-1, feature_width), flat_lists, num_segments=x_self.shape[0]
    )
    d_pre = node_grads * silu_slope(pre_act)
    d_pre_low = d_pre.astype(jnp.bfloat16)
    grad_self = dot_last(d_pre_low, w_self).astype(jnp.bfloat16)
    grad_agg = dot_last(d_pre_low, w_nbr).astype(jnp.bfloat16)
    layer_term = (
        jnp.concatenate(
            [dot_first(x_self, d_pre_low).reshape(-1), dot_first(x_agg, d_pre_low).reshape(-1)]
        )
        / pairs_dev
    )
    bias_term = (
        jnp.concatenate(
            [
                jnp.sum(d_one, axis=0),
                jnp.sum(d_two, axis=0),
                jnp.sum(loss_slope[:, None] * h_two, axis=0),
                jnp.sum(d_pre, axis=0),
            ]
        )
        / pairs_dev
    )
    bias_total = lax.psum(bias_term, ("group", "inner"))
    scorer_share, layer_share = (
        lax.psum_scatter(scorer_term, ("group", "inner"), scatter_dimension=0, tiled=True),
        lax.psum_scatter(layer_term, ("group", "inner"), scatter_dimension=0, tiled=True),
    )
    return (grad_self, grad_agg, scorer_share, layer_share, bias_total)


def solution(mesh):
    return jax.shard_map(
        body,
        mesh=mesh,
        in_specs=(
            P(("group", "inner"), None),
            P(("group", "inner"), None),
            P(),
            P(),
            P(),
            P(),
            P(),
            P(),
            P(),
            P(),
            P(("group", "inner"), None, None),
            P(("group", "inner"), None),
            P(("group", "inner"), None),
        ),
        out_specs=(
            P(("group", "inner"), None),
            P(("group", "inner"), None),
            P(("group", "inner")),
            P(("group", "inner")),
            P(),
        ),
        check_vma=False,
    )
```

profile of v0, /device:TPU:32, one launch (start us, length us, event | category | flops | bytes accessed | tf_op | source)
XLA Modules:
  0.0 595.2 jit_solution(17838501705990203355)
XLA Ops:
  7.2 0.9 compare_and_fusion
  8.1 0.9 copy.24
  9.0 0.1 copy.25
  9.1 0.1 broadcast_in_dim_reshape.7
  9.3 1.4 fusion.25
  10.7 2.5 multiply_convert_fusion.1
  13.2 13.0 %gather_fusion = bf16[3072,256]{1,0:T(8,128)(2,1)} fusion(bf16[1024,256]{1,0:T(8,128)(2,1)S(1)} %get-tuple-element.17, s32[3072]{0:T(1024)S(1)} %broadcast_clamp_fusion), kind=kCustom, calls=%fused_computation.2 | custom fusion | bytes 3158016 | tf_op jit(solution)/shard_map/jit(_take)/gather | solution.py:54
  26.1 2.3 gather.14
  28.5 0.8 broadcast_select_fusion
  29.4 0.6 copy.27
  30.0 25.7 %all_to_all.20 = bf16[8,32,12,256]{3,1,2,0:T(8,128)(2,1)S(1)} all-to-all(bf16[8,32,12,256]{3,1,2,0:T(8,128)(2,1)S(1)} %copy.27), channel_id=1, replica_groups=mesh['group'=8,'inner'=32] {'group'}, dimensions={0} | all-to-all | bytes 3145728 | tf_op jit(solution)/shard_map/all_to_all | solution.py:58
  55.6 2.1 copy.28
  57.7 11.4 %all-to-all-start.1 = ((bf16[8,32,12,256]{3,0,2,1:T(8,128)(2,1)}), bf16[8,32,12,256]{3,0,2,1:T(8,128)(2,1)S(1)}, u32[]{:S(2)}, u32[]{:S(2)}) async-start(bf16[8,32,12,256]{3,0,2,1:T(8,128)(2,1)} %copy.28), calls=%async_computation.1 | async-start | bytes 3145728 | tf_op jit(solution)/shard_map/all_to_all | solution.py:57
  69.3 37.8 %all-to-all-done.1 = bf16[8,32,12,256]{3,0,2,1:T(8,128)(2,1)S(1)} async-done(((bf16[8,32,12,256]{3,0,2,1:T(8,128)(2,1)}), bf16[8,32,12,256]{3,0,2,1:T(8,128)(2,1)S(1)}, u32[]{:S(2)}, u32[]{:S(2)}) %all-to-all-start.1) | async-done | bytes 1572896 | tf_op jit(solution)/shard_map/all_to_all | solution.py:57
  107.1 1.7 copy.29
  108.8 2.5 reshape.140
  111.3 2.0 gather_fusion.3
  113.3 2.0 gather_fusion.2
  115.2 0.2 select_convert_fusion
  115.4 7.5 %gather_fusion.1 = bf16[2048,256]{1,0:T(8,128)(2,1)S(1)} fusion(bf16[512,256]{1,0:T(8,128)(2,1)S(1)} %get-tuple-element.24, s32[2048]{0:T(1024)S(1)} %broadcast_clamp_fusion.1), kind=kCustom, calls=%fused_computation.3 | custom fusion | bytes 2105344 | tf_op jit(solution)/shard_map/jit(_take)/gather | solution.py:68
  123.0 0.4 broadcast_select_fusion.1
  123.4 0.3 fusion.1
  123.8 0.1 copy-done.8
  123.9 0.8 convolution_add_fusion
  124.8 2.9 multiply_reduce_fusion.1
  127.7 3.5 fusion.21
  131.3 2.5 fusion.24
  133.8 2.4 convert_multiply_fusion
  136.2 1.5 copy-done.3
  137.8 12.6 %scatter_custom_fusion = f32[512,256]{1,0:T(8,128)S(1)} fusion(f32[512,256]{1,0:T(8,128)S(1)} %slice.24, s32[2048]{0:T(1024)S(1)} %bitcast.65, f32[2560,256]{1,0:T(8,128)} %copy-done.3), kind=kCustom, calls=%fused_computation.21 | custom fusion | flops 524288 | bytes 2621440 | tf_op jit(solution)/shard_map/scatter-add | solution.py:95
  150.3 2.0 reduce_sum.55
  152.3 8.1 %scatter_custom_fusion.1 = f32[3072,256]{1,0:T(8,128)} fusion(s32[1024]{0:T(1024)S(1)} %bitcast.75, f32[]{:T(128)} %constant.29.clone.1, f32[512,256]{1,0:T(8,128)S(1)} %scatter_custom_fusion, f32[]{:T(128)} %constant.69, f32[512,256]{1,0:T(8,128)S(1)} %reduce_sum.55), kind=kCustom, calls=%fused_computation.25 | custom fusion | flops 524288 | bytes 4194312 | tf_op jit(solution)/shard_map/scatter-add | solution.py:98
  160.4 4.6 reshape.144
  165.0 5.6 copy.30
  170.6 4.5 all-to-all-start.2
  175.1 0.1 reshape.200
  175.2 2.6 fusion.13
  177.8 0.1 copy.38
  178.0 35.5 %all-to-all-done.2 = f32[8,32,12,256]{3,1,2,0:T(8,128)} async-done(((f32[8,32,12,256]{3,1,2,0:T(8,128)}), f32[8,32,12,256]{3,1,2,0:T(8,128)}, u32[]{:S(2)}, u32[]{:S(2)}) %all-to-all-start.2) | async-done | bytes 3145760 | tf_op jit(solution)/shard_map/all_to_all | solution.py:105
  213.5 5.4 copy.31
  218.9 6.5 %all-to-all-start.3 = ((f32[8,32,12,256]{3,0,2,1:T(8,128)}), f32[8,32,12,256]{3,0,2,1:T(8,128)}, u32[]{:S(2)}, u32[]{:S(2)}) async-start(f32[8,32,12,256]{3,0,2,1:T(8,128)} %copy.31), calls=%async_computation.3 | async-start | bytes 6291456 | tf_op jit(solution)/shard_map/all_to_all | solution.py:104
  225.5 0.3 all-reduce.5.cloned.1.call-start
  225.8 4.9 convolution_bitcast_fusion
  230.7 0.3 copy.39
  230.9 1.3 maximum_multiply_fusion
  232.3 65.1 %all-to-all-done.3 = f32[8,32,12,256]{3,0,2,1:T(8,128)} async-done(((f32[8,32,12,256]{3,0,2,1:T(8,128)}), f32[8,32,12,256]{3,0,2,1:T(8,128)}, u32[]{:S(2)}, u32[]{:S(2)}) %all-to-all-start.3) | async-done | bytes 3145760 | tf_op jit(solution)/shard_map/all_to_all | solution.py:104
  297.4 4.9 copy.32
  302.3 4.7 reshape.202
  307.0 17.7 %scatter_custom_fusion.2 = f32[1024,256]{1,0:T(8,128)S(1)} fusion(s32[3072]{0:T(1024)S(1)} %reshape.200, f32[3072,256]{1,0:T(8,128)} %reshape.202, f32[]{:T(128)} %constant.29.clone.1), kind=kCustom, calls=%fused_computation.50 | custom fusion | flops 786432 | bytes 1049088 | tf_op jit(solution)/shard_map/scatter-add | solution.py:111
  324.7 0.4 fusion.22
  325.2 0.3 convolution_bitcast_fusion.2
  325.5 0.2 copy-done.9
  325.8 0.3 convolution_bitcast_fusion.1
  326.1 0.1 copy.33
  326.3 0.1 copy.40
  326.4 0.1 copy.34
  326.5 0.1 copy.41
  326.7 0.8 maximum_multiply_fusion.1
  327.6 74.6 %psum.7 = f32[1792]{0:T(1024)} all-reduce(f32[1792]{0:T(1024)S(1)} %maximum_multiply_fusion.2), channel_id=1, replica_groups=mesh['group'=8,'inner'=32] {'group','inner'}, use_global_device_ids=true, to_apply=%region_11.13 | all-reduce | flops 1792 | bytes 14336 | tf_op jit(solution)/shard_map/psum | solution.py:135
  402.2 1.1 convolution_convert_fusion
  403.3 1.1 convolution_convert_fusion.1
  404.4 181.2 %all-reduce.5.cloned.1.call-done = (f32[393216]{0:T(1024)}, f32[131072]{0:T(1024)}) async-done(((f32[393216]{0:T(1024)}, f32[131072]{0:T(1024)}), (f32[393216]{0:T(1024)}, f32[131072]{0:T(1024)})) %all-reduce.5.cloned.1.call-update) | async-done | bytes 2097168
  585.6 1.4 dynamic-slice
  587.0 1.3 dynamic-slice.1
  (50 shorter events, 0.3 us)
Async XLA Ops:
  7.2 117.6 %copy-start = (bf16[512,512]{1,0:T(8,128)(2,1)S(1)}, bf16[512,512]{1,0:T(8,128)(2,1)}, u32[]{:S(2)}) copy-start(bf16[512,512]{1,0:T(8,128)(2,1)} %param.22) | copy-start | bytes 1572868
  55.6 13.4 %copy-start.13 = (s32[512,2]{0,1:T(2,128)S(1)}, s32[512,2]{0,1:T(2,128)}, u32[]{:S(2)}) copy-start(s32[512,2]{0,1:T(2,128)} %param.26) | copy-start | bytes 12292
  55.6 13.5 %copy-start.12 = (s32[512,4]{0,1:T(4,128)S(1)}, s32[512,4]{0,1:T(4,128)}, u32[]{:S(2)}) copy-start(s32[512,4]{0,1:T(4,128)} %param.27) | copy-start | bytes 24580
  57.7 49.4 %all-to-all-start.1 = ((bf16[8,32,12,256]{3,0,2,1:T(8,128)(2,1)}), bf16[8,32,12,256]{3,0,2,1:T(8,128)(2,1)S(1)}, u32[]{:S(2)}, u32[]{:S(2)}) async-start(bf16[8,32,12,256]{3,0,2,1:T(8,128)(2,1)} %copy.28), calls=%async_computation.1 | async-start | bytes 3145728 | tf_op jit(solution)/shard_map/all_to_all | solution.py:57
  122.9 1.0 copy-start.8
  123.0 0.9 copy-start.14
  123.9 0.9 copy-start.15
  123.9 0.9 copy-start.16
  124.8 6.5 %copy-start.2 = (f32[2560,512]{1,0:T(8,128)}, f32[2560,512]{1,0:T(8,128)S(1)}, u32[]{:S(2)}) copy-start(f32[2560,512]{1,0:T(8,128)S(1)} %convolution_add_fusion) | copy-start | bytes 15728644
  131.3 2.5 copy-start.4
  133.8 2.4 copy-start.5
  136.2 1.5 copy-start.3
  170.6 42.9 %all-to-all-start.2 = ((f32[8,32,12,256]{3,1,2,0:T(8,128)}), f32[8,32,12,256]{3,1,2,0:T(8,128)}, u32[]{:S(2)}, u32[]{:S(2)}) async-start(f32[8,32,12,256]{3,1,2,0:T(8,128)} %copy.30), calls=%async_computation.2 | async-start | bytes 6291456 | tf_op jit(solution)/shard_map/all_to_all | solution.py:105
  218.9 78.4 %all-to-all-start.3 = ((f32[8,32,12,256]{3,0,2,1:T(8,128)}), f32[8,32,12,256]{3,0,2,1:T(8,128)}, u32[]{:S(2)}, u32[]{:S(2)}) async-start(f32[8,32,12,256]{3,0,2,1:T(8,128)} %copy.31), calls=%async_computation.3 | async-start | bytes 6291456 | tf_op jit(solution)/shard_map/all_to_all | solution.py:104
  225.5 360.2 %all-reduce.5.cloned.1.call-start = ((), (), s32[]{:S(2)}) async-start(), calls=%async_computation.4 | async-start | bytes 4194304
  302.3 22.4 %copy-start.7 = (f32[1024,256]{1,0:T(8,128)S(1)}, f32[1024,256]{1,0:T(8,128)}, u32[]{:S(2)}) copy-start(f32[1024,256]{1,0:T(8,128)} %get-tuple-element.18) | copy-start | bytes 3145732
  307.0 18.2 %copy-start.6 = (bf16[1024,256]{1,0:T(8,128)(2,1)S(1)}, bf16[1024,256]{1,0:T(8,128)(2,1)}, u32[]{:S(2)}) copy-start(bf16[1024,256]{1,0:T(8,128)(2,1)} %param.15) | copy-start | bytes 1572868
  324.7 1.0 copy-start.9
  326.1 76.0 %copy-start.11 = (bf16[256,256]{1,0:T(8,128)(2,1)S(1)}, bf16[256,256]{1,0:T(8,128)(2,1)}, u32[]{:S(2)}) copy-start(bf16[256,256]{1,0:T(8,128)(2,1)} %param.18) | copy-start | bytes 393220
  326.4 76.9 %copy-start.10 = (bf16[256,256]{1,0:T(8,128)(2,1)S(1)}, bf16[256,256]{1,0:T(8,128)(2,1)}, u32[]{:S(2)}) copy-start(bf16[256,256]{1,0:T(8,128)(2,1)} %param.17) | copy-start | bytes 393220
  326.7 261.6 %copy-start.1 = (bf16[512,512]{1,0:T(8,128)(2,1)S(1)}, bf16[512,512]{1,0:T(8,128)(2,1)}, u32[]{:S(2)}) copy-start(bf16[512,512]{1,0:T(8,128)(2,1)} %param.22) | copy-start | bytes 1572868
Sparse Core Ops, SparseCore 0:
  327.7 257.8 all-reduce.4
where the time goes:
time: 599 us; the launch traced here: 595 us
  waiting for transfers between devices  320 us (53%)
  blocking collectives  100 us (17%)
  local copies, waits for them, and re-layouts  65.8 us (11%)
  other arithmetic  49.3 us (8%)
  matrix products  22.9 us (4%)
  starting transfers between devices  22.6 us (4%)
  between operations  14.6 us (2%)
    unnamed x2, waiting for transfers between devices  181 us
    psum x1, blocking collectives, body(): bias_total = lax.psum(bias_term, ('group', 'inner'))  74.6 us
    all_to_all x1, waiting for transfers between devices, body(): lax.all_to_all(lax.all_to_all(outbound, 'group', split_axis=0, concat_axi...  65.1 us
    all_to_all x1, waiting for transfers between devices, body(): lax.all_to_all(lax.all_to_all(outgoing, 'group', split_axis=0, concat_axi...  37.8 us
    all_to_all x1, waiting for transfers between devices, body(): lax.all_to_all(outbound, 'group', split_axis=0, concat_axis=0, tiled=True)  35.5 us
    all_to_all x1, blocking collectives, body(): lax.all_to_all(outgoing, 'group', split_axis=0, concat_axis=0, tiled=True)  25.7 us
    scatter-add x1, other arithmetic, body(): jax.ops.segment_sum(received.reshape(-1, feature_width), flat_lists, num_...  17.7 us
    gather x2, local copies, waits for them, and re-layouts, body(): jnp.take(node_table, flat_lists, axis=0)  15.3 us
  transfers between devices with their start and end apart: 4, of which 4 were waited for; matrix products, arithmetic and copies ran while one was open for 2% of the time, Pallas kernels for 0%

commit v1 on v0

v1 whole, which is shorter than its diff:
```python
import jax
import jax.numpy as jnp
from jax import lax
from jax.experimental import pallas as pl
from jax.experimental.pallas import tpu as pltpu
from jax.sharding import PartitionSpec as P

F32 = jnp.float32
BF16 = jnp.bfloat16


def dot(a, b):
    return jnp.dot(a, b, preferred_element_type=F32)


def dot_first(a, b):
    return lax.dot_general(a, b, (((0,), (0,)), ((), ())), preferred_element_type=F32)


def dot_last(a, b):
    return lax.dot_general(a, b, (((1,), (1,)), ((), ())), preferred_element_type=F32)


def sigm(v):
    return 0.5 + 0.5 * jnp.tanh(0.5 * v)


def one_hot(a, b):
    return jnp.where(a == b, 1.0, 0.0).astype(BF16)


def layer_kernel(xs, xa, ws, wn, bl, idx, send, slope, tab):
    nodes = xs.shape[0]
    for r in range(nodes // 256):
        rows = pl.ds(r * 256, 256)
        pre = dot(xs[rows, :], ws[...]) + dot(xa[rows, :], wn[...]) + bl[...]
        s = sigm(pre)
        t = pre * s
        tab[rows, :] = t.astype(BF16)
        slope[rows, :] = s + t * (1.0 - s)
    owners = send.shape[0]
    node_ids = lax.broadcasted_iota(jnp.int32, (256, nodes), 1)

    def full(b, carry):
        y = dot(one_hot(idx[pl.ds(b * 256, 256), :], node_ids), tab[...]).astype(BF16)
        send[pl.ds(b * 32, 32), 0:8, :] = y[:, :128].reshape(32, 8, 128)
        send[pl.ds(b * 32, 32), 8:16, :] = y[:, 128:].reshape(32, 8, 128)
        return carry

    lax.fori_loop(0, owners // 32, full, 0)
    low = lax.broadcasted_iota(jnp.int32, (256, 128), 0) % 8 < 4

    def mixed(b, carry):
        y = dot(one_hot(idx[pl.ds(owners * 8 + b * 256, 256), :], node_ids), tab[...])
        y = jnp.where(low, y[:, :128], y[:, 128:]).astype(BF16)
        send[pl.ds(b * 32, 32), 16:24, :] = y.reshape(32, 8, 128)
        return carry

    lax.fori_loop(0, owners // 32, mixed, 0)


def unpack(chunks, rows_ref):
    half = chunks.shape[0] * 8
    rows_ref[0:half, 0:128] = chunks[:, 0:8, :].reshape(half, 128)
    rows_ref[0:half, 128:256] = chunks[:, 8:16, :].reshape(half, 128)
    tail = chunks[:, 16:24, :].reshape(half, 128).astype(F32)
    rows_ref[half:, 0:128] = tail.astype(BF16)
    rows_ref[half:, 128:256] = pltpu.roll(tail, half - 4, 0).astype(BF16)


def scorer_kernel(
    chunks, pcol, plane, ncol, nlane, w1, b1, w2, b2, wo,
    out, scorer, bias,
    rows, ends, grads, split, joint, right, h1, sl1, a1, a2, d2, gw1, gw2,
):
    owners = chunks.shape[0]
    table = owners * 16
    pos = ends.shape[0] // 2
    unpack(chunks, rows)
    slot_ids = lax.broadcasted_iota(jnp.int32, (256, table), 1)

    def fetch(b, carry):
        at = pl.ds(b * 256, 256)
        ends[at, :] = dot(one_hot(pcol[at, :], slot_ids), rows[...]).astype(BF16)
        return carry

    lax.fori_loop(0, 2 * pos // 256, fetch, 0)
    src = ends.at[0:pos, :]
    dst = ends.at[pos : 2 * pos, :]
    grads[...] = jnp.zeros_like(grads)
    gw1[...] = jnp.zeros_like(gw1)
    gw2[...] = jnp.zeros_like(gw2)
    bias[...] = jnp.zeros_like(bias)
    step = 64

    def block(label):
        joint[...] = (src[...].astype(F32) * right[...].astype(F32)).astype(BF16)
        a1[...] = dot(joint[...], w1[...]) + b1[...]

        def first(c, carry):
            at = pl.ds(c * step, step)
            v = a1[at, :]
            s = sigm(v)
            h = v * s
            h1[at, :] = h.astype(BF16)
            sl1[at, :] = s + h * (1.0 - s)
            return carry

        lax.fori_loop(0, pos // step, first, 0)
        a2[...] = dot(h1[...], w2[...]) + b2[...]

        def second(c, carry):
            sum2, sumo = carry
            at = pl.ds(c * step, step)
            v = a2[at, :]
            s = sigm(v)
            h = v * s
            score = jnp.sum(h * wo[...], axis=1, keepdims=True)
            ls = sigm(score) - label
            d = ls * wo[...] * (s + h * (1.0 - s))
            d2[at, :] = d.astype(BF16)
            return (
                sum2 + jnp.sum(d.reshape(step // 8, 8, -1), axis=0),
                sumo + jnp.sum((ls * h).reshape(step // 8, 8, -1), axis=0),
            )

        zero = jnp.zeros((8, w2.shape[1]), F32)
        sum2, sumo = lax.fori_loop(0, pos // step, second, (zero, zero))
        bias[8:16, :] += sum2
        bias[16:24, :] += sumo
        a1[...] = dot_last(d2[...], w2[...])

        def third(c, carry):
            at = pl.ds(c * step, step)
            d = a1[at, :] * sl1[at, :]
            a1[at, :] = d
            return carry + jnp.sum(d.reshape(step // 8, 8, -1), axis=0)

        bias[0:8, :] += lax.fori_loop(0, pos // step, third, zero)
        d1 = a1[...].astype(BF16)
        gw1[...] += dot_first(joint[...], d1)
        gw2[...] += dot_first(h1[...], d2[...])
        dj = dot_last(d1, w1[...])
        grads[0:pos, :] += dj * right[...].astype(F32)
        return dj * src[...].astype(F32)

    right[...] = dst[...]
    grads[pos:, :] += block(1.0)
    col_ids = lax.broadcasted_iota(jnp.int32, (pos, pos), 1)
    row_ids = lax.broadcasted_iota(jnp.int32, (pos, pos), 0)

    def negative(k, carry):
        right[...] = dot(one_hot(ncol[pl.ds(k * pos, pos), :], col_ids), dst[...]).astype(BF16)
        d_right = block(0.0)
        hi = d_right.astype(BF16)
        lo = (d_right - hi.astype(F32)).astype(BF16)
        pick = one_hot(nlane[pl.ds(k, 1), :], row_ids)
        grads[pos:, :] += dot(pick, hi) + dot(pick, lo)
        return carry

    lax.fori_loop(0, nlane.shape[0], negative, 0)
    hi = grads[...].astype(BF16)
    split[:, 0:256] = hi
    split[:, 256:512] = (grads[...] - hi.astype(F32)).astype(BF16)
    sub = lax.broadcasted_iota(jnp.int32, (256, 2 * pos), 0)
    sub_mixed = sub - (sub & 4)

    def spread(ids):
        y = dot(one_hot(plane[...], ids), split[...])
        return y[:, 0:256] + y[:, 256:512]

    def full(b, carry):
        y = spread(sub + b * 256).astype(BF16)
        out[pl.ds(b * 32, 32), 0:8, :] = y[:, :128].reshape(32, 8, 128)
        out[pl.ds(b * 32, 32), 8:16, :] = y[:, 128:].reshape(32, 8, 128)
        return carry

    lax.fori_loop(0, owners // 32, full, 0)
    low = lax.broadcasted_iota(jnp.int32, (256, 128), 0) % 8 < 4

    def mixed(b, carry):
        y = spread(sub_mixed + (owners * 8 + b * 256))
        y = jnp.where(low, y[:, :128], y[:, 128:]).astype(BF16)
        out[pl.ds(b * 32, 32), 16:24, :] = y.reshape(32, 8, 128)
        return carry

    lax.fori_loop(0, owners // 32, mixed, 0)
    for g in range(8):
        for q in range(4):
            cols = slice(q * 128, q * 128 + 128)
            lo_row = g * 96
            at = q * 96
            n1 = min(max(256 - lo_row, 0), 96)
            if n1 > 0:
                scorer[g, at : at + n1, :] = gw1[lo_row : lo_row + n1, cols].astype(BF16)
            if n1 < 96:
                first_row = lo_row + n1 - 256
                scorer[g, at + n1 : at + 96, :] = gw2[first_row : first_row + 96 - n1, cols].astype(BF16)


def owner_kernel(
    chunks, lanes, slope, xs, xa, ws, wn, scorer, bias,
    gself, gagg, terms,
    rows, dpre, sums,
):
    table = lanes.shape[1]
    nodes = xs.shape[0]
    unpack(chunks, rows)
    ids = lax.broadcasted_iota(jnp.int32, (256, table), 0)

    def nodes_step(b, carry):
        at = pl.ds(b * 256, 256)
        d = dot(one_hot(lanes[...], ids + b * 256), rows[...]) * slope[at, :]
        low = d.astype(BF16)
        dpre[at, :] = low
        gself[at, :] = dot_last(low, ws[...]).astype(BF16)
        gagg[at, :] = dot_last(low, wn[...]).astype(BF16)
        return carry + jnp.sum(d.reshape(32, 8, 256), axis=0)

    total = lax.fori_loop(0, nodes // 256, nodes_step, jnp.zeros((8, 256), F32))
    total = jnp.sum(total, axis=0, keepdims=True)
    sums[...] = jnp.zeros_like(sums)
    for part in range(3):
        whole = jnp.sum(bias[part * 8 : part * 8 + 8, :], axis=0, keepdims=True)
        for q in range(4):
            sums[part * 4 + q : part * 4 + q + 1, :] = whole[:, q * 128 : q * 128 + 128]
    for q in range(2):
        sums[12 + q : 13 + q, :] = total[:, q * 128 : q * 128 + 128]
    hi = sums[0:16, :].astype(BF16)
    lo = (sums[0:16, :] - hi.astype(F32)).astype(BF16)
    parts = (dot_first(xs[...], dpre[...]), dot_first(xa[...], dpre[...]))
    for g in range(8):
        terms[g, 0:384, :] = scorer[g, :, :]
        mine = parts[g // 4]
        r = (g % 4) * 64
        for q in range(2):
            terms[g, 384 + q * 64 : 448 + q * 64, :] = mine[r : r + 64, q * 128 : q * 128 + 128].astype(BF16)
        terms[g, 512:528, :] = hi
        terms[g, 528:544, :] = lo


def body(
    x_self, x_agg, w_self, w_nbr, b_layer, w_one, b_one, w_two, b_two, w_out,
    send_lists, endpoint_slots, neg_index,
):
    nodes, width = x_self.shape
    both = ("group", "inner")
    owners = lax.axis_size("group") * lax.axis_size("inner")
    pos = endpoint_slots.shape[0]
    negs = neg_index.shape[1]
    hidden = w_one.shape[1]
    pairs = pos * (1 + negs)
    table = owners * 16
    params = pltpu.CompilerParams(vmem_limit_bytes=60 * 1024 * 1024)
    lists = send_lists.reshape(owners, 12)
    idx = jnp.concatenate(
        [lists[:, :8].reshape(-1), jnp.tile(lists[:, 8:], (1, 2)).reshape(-1)]
    ).reshape(table, 1)
    send, slope = pl.pallas_call(
        layer_kernel,
        out_shape=(
            jax.ShapeDtypeStruct((owners, 24, 128), BF16),
            jax.ShapeDtypeStruct((nodes, width), F32),
        ),
        scratch_shapes=[pltpu.VMEM((nodes, width), BF16)],
        compiler_params=params,
        name="layer",
    )(x_self, x_agg, w_self, w_nbr, b_layer.reshape(1, -1), idx)
    fetched = lax.all_to_all(send, both, 0, 0, tiled=True)
    owner = endpoint_slots // 12
    column = endpoint_slots - owner * 12
    place = jnp.where(column < 8, owner * 8 + column, owners * 8 + owner * 8 + column - 8)
    place = place.T.reshape(-1)
    neg_t = neg_index.T
    out, scorer, bias = pl.pallas_call(
        scorer_kernel,
        out_shape=(
            jax.ShapeDtypeStruct((owners, 24, 128), BF16),
            jax.ShapeDtypeStruct((8, 384, 128), BF16),
            jax.ShapeDtypeStruct((24, hidden), F32),
        ),
        scratch_shapes=[
            pltpu.VMEM((table, width), BF16),
            pltpu.VMEM((2 * pos, width), BF16),
            pltpu.VMEM((2 * pos, width), F32),
            pltpu.VMEM((2 * pos, 2 * width), BF16),
            pltpu.VMEM((pos, width), BF16),
            pltpu.VMEM((pos, width), BF16),
            pltpu.VMEM((pos, hidden), BF16),
            pltpu.VMEM((pos, hidden), F32),
            pltpu.VMEM((pos, hidden), F32),
            pltpu.VMEM((pos, hidden), F32),
            pltpu.VMEM((pos, hidden), BF16),
            pltpu.VMEM((width, hidden), F32),
            pltpu.VMEM((hidden, hidden), F32),
        ],
        compiler_params=params,
        name="scorer",
    )(
        fetched, place.reshape(-1, 1), place.reshape(1, -1), neg_t.reshape(-1, 1), neg_t,
        w_one, b_one.reshape(1, -1), w_two, b_two.reshape(1, -1), w_out.reshape(1, -1),
    )
    received = lax.all_to_all(out, both, 0, 0, tiled=True)
    lanes = jnp.concatenate(
        [
            lists[:, :8].reshape(-1),
            jnp.pad(lists[:, 8:], ((0, 0), (0, 4)), constant_values=-1).reshape(-1),
        ]
    ).reshape(1, table)
    grad_self, grad_agg, terms = pl.pallas_call(
        owner_kernel,
        out_shape=(
            jax.ShapeDtypeStruct((nodes, width), BF16),
            jax.ShapeDtypeStruct((nodes, width), BF16),
            jax.ShapeDtypeStruct((8, 544, 128), BF16),
        ),
        scratch_shapes=[
            pltpu.VMEM((table, width), BF16),
            pltpu.VMEM((nodes, width), BF16),
            pltpu.VMEM((16, 128), F32),
        ],
        compiler_params=params,
        name="owner",
    )(received, lanes, slope, x_self, x_agg, w_self, w_nbr, scorer, bias)
    near = jnp.sum(lax.all_to_all(terms, "group", 0, 0, tiled=True).astype(F32), axis=0)
    sums = near[512:528] + near[528:544]
    far = jnp.concatenate(
        [
            near[0:384].reshape(4, 32, 3, 128).transpose(1, 0, 2, 3).reshape(32, 12, 128),
            near[384:512].reshape(2, 32, 2, 128).transpose(1, 0, 2, 3).reshape(32, 4, 128),
            jnp.broadcast_to(sums[None], (32, 16, 128)),
        ],
        axis=1,
    )
    mine = jnp.sum(lax.all_to_all(far, "inner", 0, 0, tiled=True), axis=0) / pairs
    return (
        grad_self,
        grad_agg,
        mine[0:12].reshape(4, 3, 128).transpose(1, 0, 2).reshape(-1),
        mine[12:16].reshape(2, 2, 128).transpose(1, 0, 2).reshape(-1),
        mine[16:30].reshape(-1),
    )


def solution(mesh):
    both = ("group", "inner")
    return jax.shard_map(
        body,
        mesh=mesh,
        in_specs=(
            P(both, None), P(both, None), P(), P(), P(), P(), P(), P(), P(), P(),
            P(both, None, None), P(both, None), P(both, None),
        ),
        out_specs=(P(both, None), P(both, None), P(both), P(both), P()),
        check_vma=False,
    )
```

time: 599 us -> 211 us (0.35)
  waiting for transfers between devices: 320 us -> 38.5 us
  local copies, waits for them, and re-layouts: 65.8 us -> 9.38 us
  Pallas kernels: 0 us -> 54.9 us
  other arithmetic: 49.3 us -> 0.91 us
  matrix products: 22.9 us -> 0 us
  between operations: 14.6 us -> 0.82 us
  starting transfers between devices: 22.6 us -> 14.4 us
  blocking collectives: 100 us -> 91.9 us
    unnamed x2 -> x0, waiting for transfers between devices: 181 us -> none
    all_to_all x3 -> x1, waiting for transfers between devices: 138 us -> 38.5 us  [body(): fetched = lax.all_to_all(send, both, 0, 0, tiled=True)]
    psum x1 -> x0, blocking collectives: 74.6 us -> none  [body(): bias_total = lax.psum(bias_term, ('group', 'inner'))]
    all_to_all x1 -> x3, blocking collectives: 25.7 us -> 91.9 us  [the longest x1 48.6 us: body(): received = lax.all_to_all(out, both, 0, 0, tiled=True)]
    pallas_call x0 -> x3, Pallas kernels: none -> 54.9 us  [the longest x1 36.7 us: body(): pl.pallas_call(scorer_kernel, out_shape=(jax.ShapeDtypeStruct((owners, 24...]
    scatter-add x3 -> x0, other arithmetic: 38.4 us -> none  [the longest x1 17.7 us: body(): jax.ops.segment_sum(received.reshape(-1, feature_width), flat_lists, num_...]
    gather x5 -> x0, local copies, waits for them, and re-layouts: 26.7 us -> none  [the longest x2 15.3 us: body(): jnp.take(node_table, flat_lists, axis=0)]
    dot_general x12 -> x0, matrix products: 22.9 us -> none  [the longest x4 8.15 us: dot_first(): lax.dot_general(first_op, second_op, (((0,), (0,)), ((), ())), preferred_...]
  transfers between devices with their start and end apart: 4 -> 1, of which waited for: 4 -> 1; matrix products, arithmetic and copies ran while one was open for 2% -> 1% of each run, Pallas kernels for 0% -> 0%
where the time goes in v1:
time: 211 us
  blocking collectives  91.9 us (44%)
  Pallas kernels  54.9 us (26%)
  waiting for transfers between devices  38.5 us (18%)
  starting transfers between devices  14.4 us (7%)
  local copies, waits for them, and re-layouts  9.38 us (4%)
    all_to_all x1, blocking collectives, body(): received = lax.all_to_all(out, both, 0, 0, tiled=True)  48.6 us
    all_to_all x1, waiting for transfers between devices, body(): fetched = lax.all_to_all(send, both, 0, 0, tiled=True)  38.5 us
    pallas_call x1, Pallas kernels, body(): pl.pallas_call(scorer_kernel, out_shape=(jax.ShapeDtypeStruct((owners, 24...  36.7 us
    all_to_all x1, blocking collectives, body(): lax.all_to_all(far, 'inner', 0, 0, tiled=True)  23.1 us
    all_to_all x1, blocking collectives, body(): lax.all_to_all(terms, 'group', 0, 0, tiled=True).astype(F32)  20.2 us
    all_to_all x1, starting transfers between devices, body(): fetched = lax.all_to_all(send, both, 0, 0, tiled=True)  14.4 us
    pallas_call x1, Pallas kernels, body(): pl.pallas_call(layer_kernel, out_shape=(jax.ShapeDtypeStruct((owners, 24,...  10.2 us
    pallas_call x1, Pallas kernels, body(): pl.pallas_call(owner_kernel, out_shape=(jax.ShapeDtypeStruct((nodes, widt...  8.01 us
  transfers between devices with their start and end apart: 1, of which 1 were waited for; matrix products, arithmetic and copies ran while one was open for 1% of the time, Pallas kernels for 0%

profile of v1, /device:TPU:32, one launch (start us, length us, event | category | flops | bytes accessed | tf_op | source)
XLA Modules:
  0.0 210.8 jit_solution(11929851039154416167)
XLA Ops:
  0.6 0.9 copy.51
  1.6 0.1 slice.39
  1.6 0.1 reshape.75
  1.8 0.1 reshape.81
  1.9 0.1 tile.8
  2.0 0.3 tile.9
  2.3 0.6 pad_add_fusion
  2.9 2.0 copy.42.idx
  4.9 10.2 %layer.1 = (bf16[256,24,128]{2,1,0:T(8,128)(2,1)}, f32[1024,256]{1,0:T(8,128)}) custom-call(bf16[1024,256]{1,0:T(8,128)(2,1)} %xs.3, bf16[1024,256]{1,0:T(8,128)(2,1)} %xa.3, bf16[256,256]{1,0:T(8,128)(2,1)} %ws.3, bf16[256,256]{1,0:T(8,128)(2,1)} %wn.3, f32[1,256]{1,0:T(1,128)} %bitcast.58, s32[4096,1]{1,0:T(8,128)} %copy.42.idx), custom_call_target="tpu_custom_call" | custom-call | tf_op jit(solution)/shard_map/layer/pallas_call | solution.py:259
  15.1 0.0 copy-start.3
  15.1 0.0 copy-start.2
  15.1 14.4 %all-to-all-start = ((bf16[256,24,128]{2,1,0:T(8,128)(2,1)}), bf16[256,24,128]{2,1,0:T(8,128)(2,1)S(1)}, u32[]{:S(2)}, u32[]{:S(2)}) async-start(bf16[256,24,128]{2,1,0:T(8,128)(2,1)} %get-tuple-element.13), calls=%async_computation | async-start | bytes 3145728 | tf_op jit(solution)/shard_map/all_to_all | solution.py:269
  29.5 0.0 copy-done.3
  29.5 0.0 copy-start.1
  29.5 0.0 copy-done.2
  29.6 1.0 copy.53
  30.6 1.4 copy.56
  32.0 38.5 %all-to-all-done.chunks = bf16[256,24,128]{2,1,0:T(8,128)(2,1)S(1)} async-done(((bf16[256,24,128]{2,1,0:T(8,128)(2,1)}), bf16[256,24,128]{2,1,0:T(8,128)(2,1)S(1)}, u32[]{:S(2)}, u32[]{:S(2)}) %all-to-all-start) | async-done | bytes 1572896 | tf_op jit(solution)/shard_map/all_to_all | solution.py:269
  70.5 0.0 copy-start
  70.5 0.0 copy-done.1
  70.5 1.2 copy-done
  71.7 36.7 %scorer.1 = (bf16[256,24,128]{2,1,0:T(8,128)(2,1)}, bf16[8,384,128]{2,1,0:T(8,128)(2,1)}, f32[24,512]{1,0:T(8,128)}) custom-call(bf16[256,24,128]{2,1,0:T(8,128)(2,1)} %copy-done, s32[1024,1]{1,0:T(8,128)} %bitcast.38, s32[1,1024]{1,0:T(1,128)} %bitcast.48, s32[2048,1]{1,0:T(8,128)} %bitcast.37, s32[4,512]{1,0:T(4,128)} %bitcast.49, bf16[256,512]{1,0:T(8,128)(2,1)} %w1.1, ...), custom_call_target="tpu_custom_call" | custom-call | tf_op jit(solution)/shard_map/scorer/pallas_call | solution.py:275
  108.4 48.6 %all_to_all.20.chunks = bf16[256,24,128]{2,1,0:T(8,128)(2,1)} all-to-all(bf16[256,24,128]{2,1,0:T(8,128)(2,1)} %get-tuple-element.14), channel_id=1, replica_groups=mesh['group'=8,'inner'=32] {'group','inner'}, dimensions={0} | all-to-all | bytes 3145728 | tf_op jit(solution)/shard_map/all_to_all | solution.py:303
  156.9 8.0 %owner.1 = (bf16[1024,256]{1,0:T(8,128)(2,1)}, bf16[1024,256]{1,0:T(8,128)(2,1)}, bf16[8,544,128]{2,1,0:T(8,128)(2,1)}) custom-call(bf16[256,24,128]{2,1,0:T(8,128)(2,1)} %all_to_all.20.chunks, s32[1,4096]{1,0:T(1,128)} %bitcast.45, f32[1024,256]{1,0:T(8,128)} %get-tuple-element.15.slope, bf16[1024,256]{1,0:T(8,128)(2,1)} %xs.3, bf16[1024,256]{1,0:T(8,128)(2,1)} %xa.3, ...), custom_call_target="tpu_custom_call" | custom-call | tf_op jit(solution)/shard_map/owner/pallas_call | solution.py:310
  164.9 20.2 %all_to_all.21 = bf16[8,544,128]{2,1,0:T(8,128)(2,1)S(1)} all-to-all(bf16[8,544,128]{2,1,0:T(8,128)(2,1)} %get-tuple-element.20), channel_id=1, replica_groups=mesh['group'=8,'inner'=32] {'group'}, dimensions={0} | all-to-all | bytes 2228224 | tf_op jit(solution)/shard_map/all_to_all | solution.py:325
  185.2 0.2 convert_reduce_fusion
  185.5 0.1 reshape.83
  185.6 0.1 copy.47
  185.7 0.1 pad_maximum_fusion
  185.8 23.1 %all_to_all.22 = f32[32,32,128]{2,1,0:T(8,128)S(1)} all-to-all(f32[32,32,128]{2,1,0:T(8,128)S(1)} %pad_maximum_fusion), channel_id=1, replica_groups=mesh['group'=8,'inner'=32] {'inner'}, dimensions={0} | all-to-all | bytes 1048576 | tf_op jit(solution)/shard_map/all_to_all | solution.py:335
  209.0 0.6 slice_bitcast_fusion
  209.6 0.6 copy.50
  210.2 0.6 reshape.88
  (17 shorter events, 0.2 us)
Async XLA Ops:
  15.1 14.4 %copy-start.3 = (s32[512,2]{0,1:T(2,128)S(1)}, s32[512,2]{0,1:T(2,128)}, u32[]{:S(2)}) copy-start(s32[512,2]{0,1:T(2,128)} %param.24) | copy-start | bytes 12292
  15.1 14.5 %copy-start.2 = (s32[512,4]{0,1:T(4,128)S(1)}, s32[512,4]{0,1:T(4,128)}, u32[]{:S(2)}) copy-start(s32[512,4]{0,1:T(4,128)} %param.25) | copy-start | bytes 24580
  15.1 55.4 %all-to-all-start = ((bf16[256,24,128]{2,1,0:T(8,128)(2,1)}), bf16[256,24,128]{2,1,0:T(8,128)(2,1)S(1)}, u32[]{:S(2)}, u32[]{:S(2)}) async-start(bf16[256,24,128]{2,1,0:T(8,128)(2,1)} %get-tuple-element.13), calls=%async_computation | async-start | bytes 3145728 | tf_op jit(solution)/shard_map/all_to_all | solution.py:269
  29.5 41.0 %copy-start.1 = (s32[1,1,2,512]{3,1,2,0:T(1,128)}, s32[1,1,2,512]{3,1,2,0:T(1,128)S(1)}, u32[]{:S(2)}) copy-start(s32[1,1,2,512]{3,1,2,0:T(1,128)S(1)} %copy.52) | copy-start | bytes 12292
  70.5 1.2 copy-start

commit v2 on v1

v2 whole, which is shorter than its diff:
```python
import jax
import jax.numpy as jnp
from jax import lax
from jax.experimental import pallas as pl
from jax.experimental.pallas import tpu as pltpu
from jax.sharding import PartitionSpec as P

UNROLL = 16
STEP = 32
U2 = 4
PARAMS = pltpu.CompilerParams(vmem_limit_bytes=60 * 1024 * 1024)
F32 = jnp.float32
BF16 = jnp.bfloat16


def dot(a, b):
    return jnp.dot(a, b, preferred_element_type=F32)


def dot_first(a, b):
    return lax.dot_general(a, b, (((0,), (0,)), ((), ())), preferred_element_type=F32)


def dot_last(a, b):
    return lax.dot_general(a, b, (((1,), (1,)), ((), ())), preferred_element_type=F32)


def sigm(v):
    return 0.5 + 0.5 * jnp.tanh(0.5 * v)


def one_hot(a, b):
    return jnp.where(a == b, 1.0, 0.0).astype(BF16)


def column(block, offset, period):
    count, caps = block.shape
    wide = jnp.broadcast_to(block[:, None, :], (count, 8, caps)).reshape(count * 8, caps)
    want = lax.broadcasted_iota(jnp.int32, wide.shape, 0) % period + offset
    lane = lax.broadcasted_iota(jnp.int32, wide.shape, 1)
    return jnp.sum(jnp.where(lane == want, wide, 0.0), axis=1, keepdims=True)


def layer_kernel(xs, xa, ws, wn, bl, lists, send, slope, tab):
    nodes = xs.shape[0]
    for r in range(nodes // 256):
        rows = pl.ds(r * 256, 256)
        pre = dot(xs[rows, :], ws[...]) + dot(xa[rows, :], wn[...]) + bl[...]
        s = sigm(pre)
        t = pre * s
        tab[rows, :] = t.astype(BF16)
        slope[rows, :] = s + t * (1.0 - s)
    owners = send.shape[0]
    node_ids = lax.broadcasted_iota(jnp.int32, (256, nodes), 1).astype(F32)

    def full(b, carry):
        ids = column(lists[pl.ds(b * 32, 32), :].astype(F32), 0, 8)
        y = dot(one_hot(ids, node_ids), tab[...]).astype(BF16)
        send[pl.ds(b * 32, 32), 0:8, :] = y[:, :128].reshape(32, 8, 128)
        send[pl.ds(b * 32, 32), 8:16, :] = y[:, 128:].reshape(32, 8, 128)
        return carry

    lax.fori_loop(0, owners // 32, full, 0, unroll=U2)
    low = lax.broadcasted_iota(jnp.int32, (256, 128), 0) % 8 < 4

    def mixed(b, carry):
        ids = column(lists[pl.ds(b * 32, 32), :].astype(F32), 8, 4)
        y = dot(one_hot(ids, node_ids), tab[...])
        y = jnp.where(low, y[:, :128], y[:, 128:]).astype(BF16)
        send[pl.ds(b * 32, 32), 16:24, :] = y.reshape(32, 8, 128)
        return carry

    lax.fori_loop(0, owners // 32, mixed, 0, unroll=U2)


def unpack(chunks, rows_ref):
    half = chunks.shape[0] * 8
    rows_ref[0:half, 0:128] = chunks[:, 0:8, :].reshape(half, 128)
    rows_ref[0:half, 128:256] = chunks[:, 8:16, :].reshape(half, 128)
    tail = chunks[:, 16:24, :].reshape(half, 128).astype(F32)
    rows_ref[half:, 0:128] = tail.astype(BF16)
    rows_ref[half:, 128:256] = pltpu.roll(tail, half - 4, 0).astype(BF16)


def scorer_kernel(
    chunks, pcol, plane, ncol, nlane, w1, b1, w2, b2, wo,
    out, scorer, bias,
    rows, ends, grads, split, joint, right, h1, sl1, a1, a2, d1, d2, gw1, gw2,
):
    owners = chunks.shape[0]
    table = owners * 16
    pos = ends.shape[0] // 2
    unpack(chunks, rows)
    slot_ids = lax.broadcasted_iota(jnp.int32, (256, table), 1)

    def fetch(b, carry):
        at = pl.ds(b * 256, 256)
        ends[at, :] = dot(one_hot(pcol[at, :], slot_ids), rows[...]).astype(BF16)
        return carry

    lax.fori_loop(0, 2 * pos // 256, fetch, 0, unroll=U2)
    src = ends.at[0:pos, :]
    dst = ends.at[pos : 2 * pos, :]
    grads[...] = jnp.zeros_like(grads)
    gw1[...] = jnp.zeros_like(gw1)
    gw2[...] = jnp.zeros_like(gw2)
    bias[...] = jnp.zeros_like(bias)
    step = STEP

    def block(label):
        joint[...] = (src[...].astype(F32) * right[...].astype(F32)).astype(BF16)
        a1[...] = dot(joint[...], w1[...]) + b1[...]

        def first(c, carry):
            at = pl.ds(c * step, step)
            v = a1[at, :]
            s = sigm(v)
            h = v * s
            h1[at, :] = h.astype(BF16)
            sl1[at, :] = s + h * (1.0 - s)
            return carry

        lax.fori_loop(0, pos // step, first, 0, unroll=UNROLL)
        a2[...] = dot(h1[...], w2[...]) + b2[...]

        def second(c, carry):
            sum2, sumo = carry
            at = pl.ds(c * step, step)
            v = a2[at, :]
            s = sigm(v)
            h = v * s
            score = jnp.sum(h * wo[...], axis=1, keepdims=True)
            ls = sigm(score) - label
            d = ls * wo[...] * (s + h * (1.0 - s))
            d2[at, :] = d.astype(BF16)
            return (
                sum2 + jnp.sum(d.reshape(step // 8, 8, -1), axis=0),
                sumo + jnp.sum((ls * h).reshape(step // 8, 8, -1), axis=0),
            )

        zero = jnp.zeros((8, w2.shape[1]), F32)
        sum2, sumo = lax.fori_loop(0, pos // step, second, (zero, zero), unroll=UNROLL)
        bias[8:16, :] += sum2
        bias[16:24, :] += sumo
        a1[...] = dot_last(d2[...], w2[...])

        def third(c, carry):
            at = pl.ds(c * step, step)
            d = a1[at, :] * sl1[at, :]
            d1[at, :] = d.astype(BF16)
            return carry + jnp.sum(d.reshape(step // 8, 8, -1), axis=0)

        bias[0:8, :] += lax.fori_loop(0, pos // step, third, zero, unroll=UNROLL)
        gw1[...] += dot_first(joint[...], d1[...])
        gw2[...] += dot_first(h1[...], d2[...])
        dj = dot_last(d1[...], w1[...])
        grads[0:pos, :] += dj * right[...].astype(F32)
        return dj * src[...].astype(F32)

    right[...] = dst[...]
    grads[pos:, :] += block(1.0)
    col_ids = lax.broadcasted_iota(jnp.int32, (pos, pos), 1)
    row_ids = lax.broadcasted_iota(jnp.int32, (pos, pos), 0)

    def negative(k, carry):
        right[...] = dot(one_hot(ncol[pl.ds(k * pos, pos), :], col_ids), dst[...]).astype(BF16)
        d_right = block(0.0).astype(BF16)
        grads[pos:, :] += dot(one_hot(nlane[pl.ds(k, 1), :], row_ids), d_right)
        return carry

    lax.fori_loop(0, nlane.shape[0], negative, 0)
    split[...] = grads[...].astype(BF16)
    sub = lax.broadcasted_iota(jnp.int32, (256, 2 * pos), 0)
    sub_mixed = sub - (sub & 4)

    def spread(ids):
        return dot(one_hot(plane[...], ids), split[...])

    def full(b, carry):
        y = spread(sub + b * 256).astype(BF16)
        out[pl.ds(b * 32, 32), 0:8, :] = y[:, :128].reshape(32, 8, 128)
        out[pl.ds(b * 32, 32), 8:16, :] = y[:, 128:].reshape(32, 8, 128)
        return carry

    lax.fori_loop(0, owners // 32, full, 0, unroll=U2)
    low = lax.broadcasted_iota(jnp.int32, (256, 128), 0) % 8 < 4

    def mixed(b, carry):
        y = spread(sub_mixed + (owners * 8 + b * 256))
        y = jnp.where(low, y[:, :128], y[:, 128:]).astype(BF16)
        out[pl.ds(b * 32, 32), 16:24, :] = y.reshape(32, 8, 128)
        return carry

    lax.fori_loop(0, owners // 32, mixed, 0, unroll=U2)
    for g in range(8):
        for q in range(4):
            cols = slice(q * 128, q * 128 + 128)
            lo_row = g * 96
            at = q * 96
            n1 = min(max(256 - lo_row, 0), 96)
            if n1 > 0:
                scorer[g, at : at + n1, :] = gw1[lo_row : lo_row + n1, cols].astype(BF16)
            if n1 < 96:
                first_row = lo_row + n1 - 256
                scorer[g, at + n1 : at + 96, :] = gw2[first_row : first_row + 96 - n1, cols].astype(BF16)


def owner_kernel(
    chunks, lanes, slope, xs, xa, ws, wn, bias,
    gself, gagg, terms,
    rows, dpre, sums,
):
    table = lanes.shape[1]
    nodes = xs.shape[0]
    unpack(chunks, rows)
    ids = lax.broadcasted_iota(jnp.int32, (256, table), 0)

    def nodes_step(b, carry):
        at = pl.ds(b * 256, 256)
        d = dot(one_hot(lanes[...], ids + b * 256), rows[...]) * slope[at, :]
        low = d.astype(BF16)
        dpre[at, :] = low
        gself[at, :] = dot_last(low, ws[...]).astype(BF16)
        gagg[at, :] = dot_last(low, wn[...]).astype(BF16)
        return carry + jnp.sum(d.reshape(32, 8, 256), axis=0)

    total = lax.fori_loop(0, nodes // 256, nodes_step, jnp.zeros((8, 256), F32))
    total = jnp.sum(total, axis=0, keepdims=True)
    sums[...] = jnp.zeros_like(sums)
    for part in range(3):
        whole = jnp.sum(bias[part * 8 : part * 8 + 8, :], axis=0, keepdims=True)
        for q in range(4):
            sums[part * 4 + q : part * 4 + q + 1, :] = whole[:, q * 128 : q * 128 + 128]
    for q in range(2):
        sums[12 + q : 13 + q, :] = total[:, q * 128 : q * 128 + 128]
    hi = sums[0:16, :].astype(BF16)
    lo = (sums[0:16, :] - hi.astype(F32)).astype(BF16)
    parts = (dot_first(xs[...], dpre[...]), dot_first(xa[...], dpre[...]))
    for g in range(8):
        mine = parts[g // 4]
        r = (g % 4) * 64
        for q in range(2):
            terms[g, q * 64 : q * 64 + 64, :] = mine[r : r + 64, q * 128 : q * 128 + 128].astype(BF16)
        terms[g, 128:144, :] = hi
        terms[g, 144:160, :] = lo


def call_layer(*args):
    nodes, width = args[0].shape
    owners = args[5].shape[0]
    return pl.pallas_call(
        layer_kernel,
        out_shape=(
            jax.ShapeDtypeStruct((owners, 24, 128), BF16),
            jax.ShapeDtypeStruct((nodes, width), F32),
        ),
        scratch_shapes=[pltpu.VMEM((nodes, width), BF16)],
        compiler_params=PARAMS,
        name="layer",
    )(*args)


def call_scorer(*args):
    owners = args[0].shape[0]
    pos = args[2].shape[1] // 2
    table = owners * 16
    width, hidden = args[5].shape
    return pl.pallas_call(
        scorer_kernel,
        out_shape=(
            jax.ShapeDtypeStruct((owners, 24, 128), BF16),
            jax.ShapeDtypeStruct((8, 384, 128), BF16),
            jax.ShapeDtypeStruct((24, hidden), F32),
        ),
        scratch_shapes=[
            pltpu.VMEM((table, width), BF16),
            pltpu.VMEM((2 * pos, width), BF16),
            pltpu.VMEM((2 * pos, width), F32),
            pltpu.VMEM((2 * pos, width), BF16),
            pltpu.VMEM((pos, width), BF16),
            pltpu.VMEM((pos, width), BF16),
            pltpu.VMEM((pos, hidden), BF16),
            pltpu.VMEM((pos, hidden), F32),
            pltpu.VMEM((pos, hidden), F32),
            pltpu.VMEM((pos, hidden), F32),
            pltpu.VMEM((pos, hidden), BF16),
            pltpu.VMEM((pos, hidden), BF16),
            pltpu.VMEM((width, hidden), F32),
            pltpu.VMEM((hidden, hidden), F32),
        ],
        compiler_params=PARAMS,
        name="scorer",
    )(*args)


def call_owner(*args):
    nodes, width = args[3].shape
    table = args[1].shape[1]
    return pl.pallas_call(
        owner_kernel,
        out_shape=(
            jax.ShapeDtypeStruct((nodes, width), BF16),
            jax.ShapeDtypeStruct((nodes, width), BF16),
            jax.ShapeDtypeStruct((8, 160, 128), BF16),
        ),
        scratch_shapes=[
            pltpu.VMEM((table, width), BF16),
            pltpu.VMEM((nodes, width), BF16),
            pltpu.VMEM((16, 128), F32),
        ],
        compiler_params=PARAMS,
        name="owner",
    )(*args)


def body(
    x_self, x_agg, w_self, w_nbr, b_layer, w_one, b_one, w_two, b_two, w_out,
    send_lists, endpoint_slots, neg_index,
):
    nodes, width = x_self.shape
    both = ("group", "inner")
    owners = lax.axis_size("group") * lax.axis_size("inner")
    pos = endpoint_slots.shape[0]
    negs = neg_index.shape[1]
    hidden = w_one.shape[1]
    pairs = pos * (1 + negs)
    table = owners * 16
    lists = send_lists.reshape(owners, 12)
    send, slope = call_layer(x_self, x_agg, w_self, w_nbr, b_layer.reshape(1, -1), lists)
    fetched = lax.all_to_all(send, both, 0, 0, tiled=True)
    owner = endpoint_slots // 12
    column = endpoint_slots - owner * 12
    place = jnp.where(column < 8, owner * 8 + column, owners * 8 + owner * 8 + column - 8)
    place = place.T.reshape(-1)
    neg_t = neg_index.T
    out, scorer, bias = call_scorer(
        fetched, place.reshape(-1, 1), place.reshape(1, -1), neg_t.reshape(-1, 1), neg_t,
        w_one, b_one.reshape(1, -1), w_two, b_two.reshape(1, -1), w_out.reshape(1, -1),
    )
    first = jnp.sum(lax.all_to_all(scorer, "group", 0, 0, tiled=True).astype(F32), axis=0)
    first = lax.optimization_barrier(first)
    received = lax.all_to_all(out, both, 0, 0, tiled=True)
    lanes = jnp.concatenate(
        [
            lists[:, :8].reshape(-1),
            jnp.pad(lists[:, 8:], ((0, 0), (0, 4)), constant_values=-1).reshape(-1),
        ]
    ).reshape(1, table)
    grad_self, grad_agg, terms = call_owner(
        received, lanes, slope, x_self, x_agg, w_self, w_nbr, bias
    )
    near = jnp.sum(lax.all_to_all(terms, "group", 0, 0, tiled=True).astype(F32), axis=0)
    sums = near[128:144] + near[144:160]
    far = jnp.concatenate(
        [
            first.reshape(4, 32, 3, 128).transpose(1, 0, 2, 3).reshape(32, 12, 128),
            near[0:128].reshape(2, 32, 2, 128).transpose(1, 0, 2, 3).reshape(32, 4, 128),
            jnp.broadcast_to(sums[None], (32, 16, 128)),
        ],
        axis=1,
    ).astype(BF16)
    mine = jnp.sum(lax.all_to_all(far, "inner", 0, 0, tiled=True).astype(F32), axis=0) / pairs
    return (
        grad_self,
        grad_agg,
        mine[0:12].reshape(4, 3, 128).transpose(1, 0, 2).reshape(-1),
        mine[12:16].reshape(2, 2, 128).transpose(1, 0, 2).reshape(-1),
        mine[16:30].reshape(-1),
    )


def solution(mesh):
    both = ("group", "inner")
    return jax.shard_map(
        body,
        mesh=mesh,
        in_specs=(
            P(both, None), P(both, None), P(), P(), P(), P(), P(), P(), P(), P(),
            P(both, None, None), P(both, None), P(both, None),
        ),
        out_specs=(P(both, None), P(both, None), P(both), P(both), P()),
        check_vma=False,
    )
```

time: 211 us -> 184 us (0.87)
  blocking collectives: 91.9 us -> 66.2 us
  Pallas kernels: 54.9 us -> 35.9 us
  waiting for transfers between devices: 38.5 us -> 51.1 us
  starting transfers between devices: 14.4 us -> 21.5 us
    all_to_all x2 -> x1, blocking collectives: 43.3 us -> 17.6 us  [body(): lax.all_to_all(far, 'inner', 0, 0, tiled=True).astype(F32)]
    pallas_call x3, Pallas kernels: 54.9 us -> 35.9 us  [the longest x1 22.3 us: call_scorer(): pl.pallas_call(scorer_kernel, out_shape=(jax.ShapeDtypeStruct((owners, 24...]
    all_to_all x0 -> x2, waiting for transfers between devices: none -> 12.6 us  [the longest x1 7.89 us: body(): lax.all_to_all(terms, 'group', 0, 0, tiled=True).astype(F32)]
    all_to_all x0 -> x2, starting transfers between devices: none -> 7.14 us  [the longest x1 3.71 us: body(): lax.all_to_all(scorer, 'group', 0, 0, tiled=True).astype(F32)]
    reshape x5 -> x3, local copies, waits for them, and re-layouts: 3.15 us -> 0.11 us  [the longest x2 0.1 us: body(): first.reshape(4, 32, 3, 128).transpose(1, 0, 2, 3).reshape(32, 12, 128)]
    unnamed x12 -> x15, local copies, waits for them, and re-layouts: 3.62 us -> 5.13 us
  transfers between devices with their start and end apart: 1 -> 3, of which waited for: 1 -> 3; matrix products, arithmetic and copies ran while one was open for 1% -> 2% of each run, Pallas kernels for 0% -> 4%
where the time goes in v2:
time: 184 us
  blocking collectives  66.2 us (36%)
  waiting for transfers between devices  51.1 us (28%)
  Pallas kernels  35.9 us (20%)
  starting transfers between devices  21.5 us (12%)
  local copies, waits for them, and re-layouts  7.42 us (4%)
    all_to_all x1, blocking collectives, body(): received = lax.all_to_all(out, both, 0, 0, tiled=True)  48.6 us
    all_to_all x1, waiting for transfers between devices, body(): fetched = lax.all_to_all(send, both, 0, 0, tiled=True)  38.5 us
    pallas_call x1, Pallas kernels, call_scorer(): pl.pallas_call(scorer_kernel, out_shape=(jax.ShapeDtypeStruct((owners, 24...  22.3 us
    all_to_all x1, blocking collectives, body(): lax.all_to_all(far, 'inner', 0, 0, tiled=True).astype(F32)  17.6 us
    all_to_all x1, starting transfers between devices, body(): fetched = lax.all_to_all(send, both, 0, 0, tiled=True)  14.4 us
    all_to_all x1, waiting for transfers between devices, body(): lax.all_to_all(terms, 'group', 0, 0, tiled=True).astype(F32)  7.89 us
    pallas_call x1, Pallas kernels, call_owner(): pl.pallas_call(owner_kernel, out_shape=(jax.ShapeDtypeStruct((nodes, widt...  7.49 us
    pallas_call x1, Pallas kernels, call_layer(): pl.pallas_call(layer_kernel, out_shape=(jax.ShapeDtypeStruct((owners, 24,...  6.13 us
  transfers between devices with their start and end apart: 3, of which 3 were waited for; matrix products, arithmetic and copies ran while one was open for 2% of the time, Pallas kernels for 4%

profile of v2, /device:TPU:32, one launch (start us, length us, event | category | flops | bytes accessed | tf_op | source)
XLA Modules:
  0.0 183.9 jit_solution(6319308485435350735)
XLA Ops:
  0.6 1.6 copy.36
  2.2 6.1 %layer.1 = (bf16[256,24,128]{2,1,0:T(8,128)(2,1)}, f32[1024,256]{1,0:T(8,128)}) custom-call(bf16[1024,256]{1,0:T(8,128)(2,1)} %xs.3, bf16[1024,256]{1,0:T(8,128)(2,1)} %xa.3, bf16[256,256]{1,0:T(8,128)(2,1)} %ws.3, bf16[256,256]{1,0:T(8,128)(2,1)} %wn.3, f32[1,256]{1,0:T(1,128)} %bitcast.57, s32[256,12]{1,0:T(8,128)} %bitcast.38), custom_call_target="tpu_custom_call" | custom-call | tf_op jit(solution)/shard_map/layer/pallas_call | solution.py:251
  8.3 0.0 copy-start.4
  8.3 0.0 copy-start.3
  8.3 14.4 %all-to-all-start = ((bf16[256,24,128]{2,1,0:T(8,128)(2,1)}), bf16[256,24,128]{2,1,0:T(8,128)(2,1)S(1)}, u32[]{:S(2)}, u32[]{:S(2)}) async-start(bf16[256,24,128]{2,1,0:T(8,128)(2,1)} %get-tuple-element.13), calls=%async_computation | async-start | bytes 3145728 | tf_op jit(solution)/shard_map/all_to_all | solution.py:330
  22.7 0.0 copy-done.4
  22.8 0.0 copy-start.2
  22.8 0.0 copy-done.3
  22.8 1.0 copy.46
  23.9 1.4 copy.49
  25.2 38.5 %all-to-all-done.chunks = bf16[256,24,128]{2,1,0:T(8,128)(2,1)S(1)} async-done(((bf16[256,24,128]{2,1,0:T(8,128)(2,1)}), bf16[256,24,128]{2,1,0:T(8,128)(2,1)S(1)}, u32[]{:S(2)}, u32[]{:S(2)}) %all-to-all-start) | async-done | bytes 1572896 | tf_op jit(solution)/shard_map/all_to_all | solution.py:330
  63.8 0.0 copy-start
  63.8 0.0 copy-done.2
  63.8 1.1 copy-done
  64.9 22.3 %scorer.1 = (bf16[256,24,128]{2,1,0:T(8,128)(2,1)}, bf16[8,384,128]{2,1,0:T(8,128)(2,1)}, f32[24,512]{1,0:T(8,128)}) custom-call(bf16[256,24,128]{2,1,0:T(8,128)(2,1)} %copy-done, s32[1024,1]{1,0:T(8,128)} %bitcast.37, s32[1,1024]{1,0:T(1,128)} %bitcast.47, s32[2048,1]{1,0:T(8,128)} %bitcast.36, s32[4,512]{1,0:T(4,128)} %bitcast.48, bf16[256,512]{1,0:T(8,128)(2,1)} %w1.1, ...), custom_call_target="tpu_custom_call" | custom-call | tf_op jit(solution)/shard_map/scorer/pallas_call | solution.py:268
  87.2 48.6 %all_to_all.25.chunks = bf16[256,24,128]{2,1,0:T(8,128)(2,1)} all-to-all(bf16[256,24,128]{2,1,0:T(8,128)(2,1)} %get-tuple-element.14), channel_id=1, replica_groups=mesh['group'=8,'inner'=32] {'group','inner'}, dimensions={0} | all-to-all | bytes 3145728 | tf_op jit(solution)/shard_map/all_to_all | solution.py:342
  135.7 0.0 copy-start.1
  135.8 3.7 %all-to-all-start.2 = ((bf16[8,384,128]{2,1,0:T(8,128)(2,1)}), bf16[8,384,128]{2,1,0:T(8,128)(2,1)S(1)}, u32[]{:S(2)}, u32[]{:S(2)}) async-start(bf16[8,384,128]{2,1,0:T(8,128)(2,1)} %get-tuple-element.19), calls=%async_computation.2 | async-start | bytes 1572864 | tf_op jit(solution)/shard_map/all_to_all | solution.py:340
  139.5 0.0 copy-done.1
  139.5 0.1 slice.34
  139.6 0.1 reshape.75
  139.7 0.1 reshape.76
  139.8 0.6 pad_add_fusion
  140.4 7.5 %owner.1 = (bf16[1024,256]{1,0:T(8,128)(2,1)}, bf16[1024,256]{1,0:T(8,128)(2,1)}, bf16[8,160,128]{2,1,0:T(8,128)(2,1)}) custom-call(bf16[256,24,128]{2,1,0:T(8,128)(2,1)} %all_to_all.25.chunks, s32[1,4096]{1,0:T(1,128)} %bitcast.45, f32[1024,256]{1,0:T(8,128)} %get-tuple-element.15.slope, bf16[1024,256]{1,0:T(8,128)(2,1)} %xs.3, bf16[1024,256]{1,0:T(8,128)(2,1)} %xa.3, ...), custom_call_target="tpu_custom_call" | custom-call | tf_op jit(solution)/shard_map/owner/pallas_call | solution.py:299
  147.9 4.7 %all-to-all-done.2 = bf16[8,384,128]{2,1,0:T(8,128)(2,1)S(1)} async-done(((bf16[8,384,128]{2,1,0:T(8,128)(2,1)}), bf16[8,384,128]{2,1,0:T(8,128)(2,1)S(1)}, u32[]{:S(2)}, u32[]{:S(2)}) %all-to-all-start.2) | async-done | bytes 786464 | tf_op jit(solution)/shard_map/all_to_all | solution.py:340
  152.6 3.4 %all-to-all-start.3 = ((bf16[8,160,128]{2,1,0:T(8,128)(2,1)}), bf16[8,160,128]{2,1,0:T(8,128)(2,1)S(1)}, u32[]{:S(2)}, u32[]{:S(2)}) async-start(bf16[8,160,128]{2,1,0:T(8,128)(2,1)} %get-tuple-element.20), calls=%async_computation.3 | async-start | bytes 655360 | tf_op jit(solution)/shard_map/all_to_all | solution.py:352
  156.0 0.1 convert_reduce_fusion
  156.1 0.1 reshape.78
  156.3 7.9 %all-to-all-done.3 = bf16[8,160,128]{2,1,0:T(8,128)(2,1)S(1)} async-done(((bf16[8,160,128]{2,1,0:T(8,128)(2,1)}), bf16[8,160,128]{2,1,0:T(8,128)(2,1)S(1)}, u32[]{:S(2)}, u32[]{:S(2)}) %all-to-all-start.3) | async-done | bytes 327712 | tf_op jit(solution)/shard_map/all_to_all | solution.py:352
  164.3 0.1 pad_maximum_fusion
  164.4 17.6 %all_to_all.26 = bf16[32,32,128]{2,1,0:T(8,128)(2,1)S(1)} all-to-all(bf16[32,32,128]{2,1,0:T(8,128)(2,1)S(1)} %pad_maximum_fusion), channel_id=1, replica_groups=mesh['group'=8,'inner'=32] {'inner'}, dimensions={0} | all-to-all | bytes 524288 | tf_op jit(solution)/shard_map/all_to_all | solution.py:362
  182.1 0.6 slice_bitcast_fusion
  182.7 0.6 copy.44
  183.3 0.6 reshape.83
  (18 shorter events, 0.3 us)
Async XLA Ops:
  8.3 14.4 %copy-start.4 = (s32[512,2]{0,1:T(2,128)S(1)}, s32[512,2]{0,1:T(2,128)}, u32[]{:S(2)}) copy-start(s32[512,2]{0,1:T(2,128)} %param.24) | copy-start | bytes 12292
  8.3 14.5 %copy-start.3 = (s32[512,4]{0,1:T(4,128)S(1)}, s32[512,4]{0,1:T(4,128)}, u32[]{:S(2)}) copy-start(s32[512,4]{0,1:T(4,128)} %param.25) | copy-start | bytes 24580
  8.3 55.4 %all-to-all-start = ((bf16[256,24,128]{2,1,0:T(8,128)(2,1)}), bf16[256,24,128]{2,1,0:T(8,128)(2,1)S(1)}, u32[]{:S(2)}, u32[]{:S(2)}) async-start(bf16[256,24,128]{2,1,0:T(8,128)(2,1)} %get-tuple-element.13), calls=%async_computation | async-start | bytes 3145728 | tf_op jit(solution)/shard_map/all_to_all | solution.py:330
  22.8 41.0 %copy-start.2 = (s32[1,1,2,512]{3,1,2,0:T(1,128)}, s32[1,1,2,512]{3,1,2,0:T(1,128)S(1)}, u32[]{:S(2)}) copy-start(s32[1,1,2,512]{3,1,2,0:T(1,128)S(1)} %copy.45) | copy-start | bytes 12292
  63.8 1.1 copy-start
  135.7 3.7 %copy-start.1 = (s32[8,32,12]{2,1,0:T(8,128)S(1)}, s32[8,32,12]{2,1,0:T(8,128)}, u32[]{:S(2)}) copy-start(s32[8,32,12]{2,1,0:T(8,128)} %copy.36) | copy-start | bytes 36868
  135.8 16.8 %all-to-all-start.2 = ((bf16[8,384,128]{2,1,0:T(8,128)(2,1)}), bf16[8,384,128]{2,1,0:T(8,128)(2,1)S(1)}, u32[]{:S(2)}, u32[]{:S(2)}) async-start(bf16[8,384,128]{2,1,0:T(8,128)(2,1)} %get-tuple-element.19), calls=%async_computation.2 | async-start | bytes 1572864 | tf_op jit(solution)/shard_map/all_to_all | solution.py:340
  152.6 11.6 %all-to-all-start.3 = ((bf16[8,160,128]{2,1,0:T(8,128)(2,1)}), bf16[8,160,128]{2,1,0:T(8,128)(2,1)S(1)}, u32[]{:S(2)}, u32[]{:S(2)}) async-start(bf16[8,160,128]{2,1,0:T(8,128)(2,1)} %get-tuple-element.20), calls=%async_computation.3 | async-start | bytes 655360 | tf_op jit(solution)/shard_map/all_to_all | solution.py:352

commit v3 on v2

--- a/solution.py
+++ b/solution.py
@@ -8,7 +8,7 @@
 UNROLL = 16
 STEP = 32
 U2 = 4
-PARAMS = pltpu.CompilerParams(vmem_limit_bytes=60 * 1024 * 1024)
+PARAMS = pltpu.CompilerParams(vmem_limit_bytes=36 * 1024 * 1024)
 F32 = jnp.float32
 BF16 = jnp.bfloat16
 
@@ -53,24 +53,16 @@
     owners = send.shape[0]
     node_ids = lax.broadcasted_iota(jnp.int32, (256, nodes), 1).astype(F32)
 
-    def full(b, carry):
-        ids = column(lists[pl.ds(b * 32, 32), :].astype(F32), 0, 8)
-        y = dot(one_hot(ids, node_ids), tab[...]).astype(BF16)
-        send[pl.ds(b * 32, 32), 0:8, :] = y[:, :128].reshape(32, 8, 128)
-        send[pl.ds(b * 32, 32), 8:16, :] = y[:, 128:].reshape(32, 8, 128)
-        return carry
-
-    lax.fori_loop(0, owners // 32, full, 0, unroll=U2)
     low = lax.broadcasted_iota(jnp.int32, (256, 128), 0) % 8 < 4
-
-    def mixed(b, carry):
-        ids = column(lists[pl.ds(b * 32, 32), :].astype(F32), 8, 4)
-        y = dot(one_hot(ids, node_ids), tab[...])
+    for b in range(owners // 32):
+        mine = jnp.transpose(lists[:, b, :].astype(F32))
+        at = slice(b * 32, b * 32 + 32)
+        y = dot(one_hot(column(mine, 0, 8), node_ids), tab[...]).astype(BF16)
+        send[at, 0:8, :] = y[:, :128].reshape(32, 8, 128)
+        send[at, 8:16, :] = y[:, 128:].reshape(32, 8, 128)
+        y = dot(one_hot(column(mine, 8, 4), node_ids), tab[...])
         y = jnp.where(low, y[:, :128], y[:, 128:]).astype(BF16)
-        send[pl.ds(b * 32, 32), 16:24, :] = y.reshape(32, 8, 128)
-        return carry
-
-    lax.fori_loop(0, owners // 32, mixed, 0, unroll=U2)
+        send[at, 16:24, :] = y.reshape(32, 8, 128)
 
 
 def unpack(chunks, rows_ref):
@@ -82,37 +74,17 @@
     rows_ref[half:, 128:256] = pltpu.roll(tail, half - 4, 0).astype(BF16)
 
 
-def scorer_kernel(
-    chunks, pcol, plane, ncol, nlane, w1, b1, w2, b2, wo,
-    out, scorer, bias,
-    rows, ends, grads, split, joint, right, h1, sl1, a1, a2, d1, d2, gw1, gw2,
-):
-    owners = chunks.shape[0]
-    table = owners * 16
+def pair_blocks(ends, right, joint, h1, sl1, a1, a2, d1, d2, ncol, nlane, w1, b1, w2, b2, wo, grads, gw1, gw2, bias):
     pos = ends.shape[0] // 2
-    unpack(chunks, rows)
-    slot_ids = lax.broadcasted_iota(jnp.int32, (256, table), 1)
-
-    def fetch(b, carry):
-        at = pl.ds(b * 256, 256)
-        ends[at, :] = dot(one_hot(pcol[at, :], slot_ids), rows[...]).astype(BF16)
-        return carry
-
-    lax.fori_loop(0, 2 * pos // 256, fetch, 0, unroll=U2)
     src = ends.at[0:pos, :]
     dst = ends.at[pos : 2 * pos, :]
-    grads[...] = jnp.zeros_like(grads)
-    gw1[...] = jnp.zeros_like(gw1)
-    gw2[...] = jnp.zeros_like(gw2)
-    bias[...] = jnp.zeros_like(bias)
-    step = STEP
 
     def block(label):
         joint[...] = (src[...].astype(F32) * right[...].astype(F32)).astype(BF16)
         a1[...] = dot(joint[...], w1[...]) + b1[...]
 
         def first(c, carry):
-            at = pl.ds(c * step, step)
+            at = pl.ds(c * STEP, STEP)
             v = a1[at, :]
             s = sigm(v)
             h = v * s
@@ -120,12 +92,15 @@
             sl1[at, :] = s + h * (1.0 - s)
             return carry
 
-        lax.fori_loop(0, pos // step, first, 0, unroll=UNROLL)
+        lax.fori_loop(0, pos // STEP, first, 0, unroll=UNROLL)
         a2[...] = dot(h1[...], w2[...]) + b2[...]
+        zero = jnp.zeros((8, w2.shape[1]), F32)
+
+        def fold(d):
+            return jnp.sum(d.reshape(STEP // 8, 8, -1), axis=0)
 
         def second(c, carry):
-            sum2, sumo = carry
-            at = pl.ds(c * step, step)
+            at = pl.ds(c * STEP, STEP)
             v = a2[at, :]
             s = sigm(v)
             h = v * s
@@ -133,42 +108,71 @@
             ls = sigm(score) - label
             d = ls * wo[...] * (s + h * (1.0 - s))
             d2[at, :] = d.astype(BF16)
-            return (
-                sum2 + jnp.sum(d.reshape(step // 8, 8, -1), axis=0),
-                sumo + jnp.sum((ls * h).reshape(step // 8, 8, -1), axis=0),
-            )
-
-        zero = jnp.zeros((8, w2.shape[1]), F32)
-        sum2, sumo = lax.fori_loop(0, pos // step, second, (zero, zero), unroll=UNROLL)
-        bias[8:16, :] += sum2
-        bias[16:24, :] += sumo
+            if grads is not None:
+                return carry
+            return (carry[0] + fold(d), carry[1] + fold(ls * h))
+
+        start = 0 if grads is not None else (zero, zero)
+        sums = lax.fori_loop(0, pos // STEP, second, start, unroll=UNROLL)
         a1[...] = dot_last(d2[...], w2[...])
 
         def third(c, carry):
-            at = pl.ds(c * step, step)
+            at = pl.ds(c * STEP, STEP)
             d = a1[at, :] * sl1[at, :]
             d1[at, :] = d.astype(BF16)
-            return carry + jnp.sum(d.reshape(step // 8, 8, -1), axis=0)
-
-        bias[0:8, :] += lax.fori_loop(0, pos // step, third, zero, unroll=UNROLL)
-        gw1[...] += dot_first(joint[...], d1[...])
-        gw2[...] += dot_first(h1[...], d2[...])
+            return carry if grads is not None else carry + fold(d)
+
+        start = 0 if grads is not None else zero
+        sum1 = lax.fori_loop(0, pos // STEP, third, start, unroll=UNROLL)
+        if grads is None:
+            bias[0:8, :] += sum1
+            bias[8:16, :] += sums[0]
+            bias[16:24, :] += sums[1]
+            gw1[...] += dot_first(joint[...], d1[...])
+            gw2[...] += dot_first(h1[...], d2[...])
+            return None
         dj = dot_last(d1[...], w1[...])
         grads[0:pos, :] += dj * right[...].astype(F32)
         return dj * src[...].astype(F32)
 
     right[...] = dst[...]
-    grads[pos:, :] += block(1.0)
+    d_right = block(1.0)
+    if grads is not None:
+        grads[pos:, :] += d_right
     col_ids = lax.broadcasted_iota(jnp.int32, (pos, pos), 1)
     row_ids = lax.broadcasted_iota(jnp.int32, (pos, pos), 0)
 
     def negative(k, carry):
         right[...] = dot(one_hot(ncol[pl.ds(k * pos, pos), :], col_ids), dst[...]).astype(BF16)
-        d_right = block(0.0).astype(BF16)
-        grads[pos:, :] += dot(one_hot(nlane[pl.ds(k, 1), :], row_ids), d_right)
+        d_right = block(0.0)
+        if grads is not None:
+            grads[pos:, :] += dot(one_hot(nlane[pl.ds(k, 1), :], row_ids), d_right.astype(BF16))
         return carry
 
-    lax.fori_loop(0, nlane.shape[0], negative, 0)
+    lax.fori_loop(0, ncol.shape[0] // pos, negative, 0)
+
+
+def slots_kernel(
+    chunks, pcol, plane, ncol, nlane, w1, b1, w2, b2, wo,
+    out, ends,
+    rows, grads, split, right, joint, h1, sl1, a1, a2, d1, d2,
+):
+    owners = chunks.shape[0]
+    table = owners * 16
+    pos = ends.shape[0] // 2
+    unpack(chunks, rows)
+    slot_ids = lax.broadcasted_iota(jnp.int32, (256, table), 1)
+
+    def fetch(b, carry):
+        at = pl.ds(b * 256, 256)
+        ends[at, :] = dot(one_hot(pcol[at, :], slot_ids), rows[...]).astype(BF16)
+        return carry
+
+    lax.fori_loop(0, 2 * pos // 256, fetch, 0, unroll=U2)
+    grads[...] = jnp.zeros_like(grads)
+    pair_blocks(
+        ends, right, joint, h1, sl1, a1, a2, d1, d2, ncol, nlane, w1, b1, w2, b2, wo, grads, None, None, None
+    )
     split[...] = grads[...].astype(BF16)
     sub = lax.broadcasted_iota(jnp.int32, (256, 2 * pos), 0)
     sub_mixed = sub - (sub & 4)
@@ -192,6 +196,19 @@
         return carry
 
     lax.fori_loop(0, owners // 32, mixed, 0, unroll=U2)
+
+
+def weights_kernel(
+    ends, ncol, w1, b1, w2, b2, wo,
+    scorer, bias,
+    right, joint, h1, sl1, a1, a2, d1, d2, gw1, gw2,
+):
+    gw1[...] = jnp.zeros_like(gw1)
+    gw2[...] = jnp.zeros_like(gw2)
+    bias[...] = jnp.zeros_like(bias)
+    pair_blocks(
+        ends, right, joint, h1, sl1, a1, a2, d1, d2, ncol, None, w1, b1, w2, b2, wo, None, gw1, gw2, bias
+    )
     for g in range(8):
         for q in range(4):
             cols = slice(q * 128, q * 128 + 128)
@@ -206,9 +223,9 @@
 
 
 def owner_kernel(
-    chunks, lanes, slope, xs, xa, ws, wn, bias,
-    gself, gagg, terms,
-    rows, dpre, sums,
+    chunks, lanes, slope, xs, xa, bias,
+    dpre, terms,
+    rows, sums,
 ):
     table = lanes.shape[1]
     nodes = xs.shape[0]
@@ -220,8 +237,6 @@
         d = dot(one_hot(lanes[...], ids + b * 256), rows[...]) * slope[at, :]
         low = d.astype(BF16)
         dpre[at, :] = low
-        gself[at, :] = dot_last(low, ws[...]).astype(BF16)
-        gagg[at, :] = dot_last(low, wn[...]).astype(BF16)
         return carry + jnp.sum(d.reshape(32, 8, 256), axis=0)
 
     total = lax.fori_loop(0, nodes // 256, nodes_step, jnp.zeros((8, 256), F32))
@@ -245,9 +260,14 @@
         terms[g, 144:160, :] = lo
 
 
+def inputs_kernel(dpre, ws, wn, gself, gagg):
+    gself[...] = dot_last(dpre[...], ws[...]).astype(BF16)
+    gagg[...] = dot_last(dpre[...], wn[...]).astype(BF16)
+
+
 def call_layer(*args):
     nodes, width = args[0].shape
-    owners = args[5].shape[0]
+    owners = args[5].shape[1] * args[5].shape[2]
     return pl.pallas_call(
         layer_kernel,
         out_shape=(
@@ -260,36 +280,53 @@
     )(*args)
 
 
-def call_scorer(*args):
+def block_scratch(pos, width, hidden):
+    return [
+        pltpu.VMEM((pos, width), BF16),
+        pltpu.VMEM((pos, width), BF16),
+        pltpu.VMEM((pos, hidden), BF16),
+        pltpu.VMEM((pos, hidden), F32),
+        pltpu.VMEM((pos, hidden), F32),
+        pltpu.VMEM((pos, hidden), F32),
+        pltpu.VMEM((pos, hidden), BF16),
+        pltpu.VMEM((pos, hidden), BF16),
+    ]
+
+
+def call_slots(*args):
     owners = args[0].shape[0]
     pos = args[2].shape[1] // 2
-    table = owners * 16
     width, hidden = args[5].shape
     return pl.pallas_call(
-        scorer_kernel,
+        slots_kernel,
         out_shape=(
             jax.ShapeDtypeStruct((owners, 24, 128), BF16),
+            jax.ShapeDtypeStruct((2 * pos, width), BF16),
+        ),
+        scratch_shapes=[
+            pltpu.VMEM((owners * 16, width), BF16),
+            pltpu.VMEM((2 * pos, width), F32),
+            pltpu.VMEM((2 * pos, width), BF16),
+        ]
+        + block_scratch(pos, width, hidden),
+        compiler_params=PARAMS,
+        name="slots",
+    )(*args)
+
+
+def call_weights(*args):
+    pos = args[0].shape[0] // 2
+    width, hidden = args[2].shape
+    return pl.pallas_call(
+        weights_kernel,
+        out_shape=(
             jax.ShapeDtypeStruct((8, 384, 128), BF16),
             jax.ShapeDtypeStruct((24, hidden), F32),
         ),
-        scratch_shapes=[
-            pltpu.VMEM((table, width), BF16),
-            pltpu.VMEM((2 * pos, width), BF16),
-            pltpu.VMEM((2 * pos, width), F32),
-            pltpu.VMEM((2 * pos, width), BF16),
-            pltpu.VMEM((pos, width), BF16),
-            pltpu.VMEM((pos, width), BF16),
-            pltpu.VMEM((pos, hidden), BF16),
-            pltpu.VMEM((pos, hidden), F32),
-            pltpu.VMEM((pos, hidden), F32),
-            pltpu.VMEM((pos, hidden), F32),
-            pltpu.VMEM((pos, hidden), BF16),
-            pltpu.VMEM((pos, hidden), BF16),
-            pltpu.VMEM((width, hidden), F32),
-            pltpu.VMEM((hidden, hidden), F32),
-        ],
+        scratch_shapes=block_scratch(pos, width, hidden)
+        + [pltpu.VMEM((width, hidden), F32), pltpu.VMEM((hidden, hidden), F32)],
         compiler_params=PARAMS,
-        name="scorer",
+        name="weights",
     )(*args)
 
 
@@ -300,17 +337,28 @@
         owner_kernel,
         out_shape=(
             jax.ShapeDtypeStruct((nodes, width), BF16),
-            jax.ShapeDtypeStruct((nodes, width), BF16),
             jax.ShapeDtypeStruct((8, 160, 128), BF16),
         ),
-        scratch_shapes=[
-            pltpu.VMEM((table, width), BF16),
-            pltpu.VMEM((nodes, width), BF16),
-            pltpu.VMEM((16, 128), F32),
-        ],
+        scratch_shapes=[pltpu.VMEM((table, width), BF16), pltpu.VMEM((16, 128), F32)],
         compiler_params=PARAMS,
         name="owner",
     )(*args)
+
+
+def call_inputs(*args):
+    return pl.pallas_call(
+        inputs_kernel,
+        out_shape=(
+            jax.ShapeDtypeStruct(args[0].shape, BF16),
+            jax.ShapeDtypeStruct(args[0].shape, BF16),
+        ),
+        compiler_params=PARAMS,
+        name="inputs",
+    )(*args)
+
+
+def near_core(x):
+    return pltpu.with_memory_space_constraint(x, pltpu.VMEM)
 
 
 def body(
@@ -326,29 +374,28 @@
     pairs = pos * (1 + negs)
     table = owners * 16
     lists = send_lists.reshape(owners, 12)
-    send, slope = call_layer(x_self, x_agg, w_self, w_nbr, b_layer.reshape(1, -1), lists)
-    fetched = lax.all_to_all(send, both, 0, 0, tiled=True)
+    send, slope = call_layer(x_self, x_agg, w_self, w_nbr, b_layer.reshape(1, -1), send_lists.transpose(2, 0, 1))
+    fetched = near_core(lax.all_to_all(send, both, 0, 0, tiled=True))
     owner = endpoint_slots // 12
     column = endpoint_slots - owner * 12
     place = jnp.where(column < 8, owner * 8 + column, owners * 8 + owner * 8 + column - 8)
     place = place.T.reshape(-1)
     neg_t = neg_index.T
-    out, scorer, bias = call_scorer(
-        fetched, place.reshape(-1, 1), place.reshape(1, -1), neg_t.reshape(-1, 1), neg_t,
-        w_one, b_one.reshape(1, -1), w_two, b_two.reshape(1, -1), w_out.reshape(1, -1),
-    )
+    ncol = neg_t.reshape(-1, 1)
+    scorer_args = (w_one, b_one.reshape(1, -1), w_two, b_two.reshape(1, -1), w_out.reshape(1, -1))
+    out, ends = call_slots(fetched, place.reshape(-1, 1), place.reshape(1, -1), ncol, neg_t, *scorer_args)
+    scorer, bias = call_weights(ends, ncol, *scorer_args)
     first = jnp.sum(lax.all_to_all(scorer, "group", 0, 0, tiled=True).astype(F32), axis=0)
     first = lax.optimization_barrier(first)
-    received = lax.all_to_all(out, both, 0, 0, tiled=True)
+    received = near_core(lax.all_to_all(out, both, 0, 0, tiled=True))
     lanes = jnp.concatenate(
         [
             lists[:, :8].reshape(-1),
             jnp.pad(lists[:, 8:], ((0, 0), (0, 4)), constant_values=-1).reshape(-1),
         ]
     ).reshape(1, table)
-    grad_self, grad_agg, terms = call_owner(
-        received, lanes, slope, x_self, x_agg, w_self, w_nbr, bias
-    )
+    d_pre, terms = call_owner(received, lanes, slope, x_self, x_agg, bias)
+    grad_self, grad_agg = call_inputs(d_pre, w_self, w_nbr)
     near = jnp.sum(lax.all_to_all(terms, "group", 0, 0, tiled=True).astype(F32), axis=0)
     sums = near[128:144] + near[144:160]
     far = jnp.concatenate(

time: 184 us -> 184 us (level)
  blocking collectives: 66.2 us -> 0 us
  waiting for transfers between devices: 51.1 us -> 92.1 us
  starting transfers between devices: 21.5 us -> 35.7 us
  local copies, waits for them, and re-layouts: 7.42 us -> 16.3 us
    all_to_all x2 -> x0, blocking collectives: 66.2 us -> none  [the longest x1 48.6 us: body(): received = lax.all_to_all(out, both, 0, 0, tiled=True)]
    all_to_all x1 -> x3, waiting for transfers between devices: 38.5 us -> 78.5 us  [the longest x1 40.3 us: body(): fetched = near_core(lax.all_to_all(send, both, 0, 0, tiled=True))]
    all_to_all x1 -> x3, starting transfers between devices: 14.4 us -> 28.1 us  [the longest x1 14.4 us: body(): fetched = near_core(lax.all_to_all(send, both, 0, 0, tiled=True))]
    unnamed x15 -> x56, local copies, waits for them, and re-layouts: 5.13 us -> 13.9 us
    pallas_call x1 -> x3, Pallas kernels: 22.3 us -> 28.3 us  [the longest x1 15.8 us: call_slots(): pl.pallas_call(slots_kernel, out_shape=(jax.ShapeDtypeStruct((owners, 24,...]
    pallas_call x1, Pallas kernels: 7.49 us -> 3.72 us  [call_owner(): pl.pallas_call(owner_kernel, out_shape=(jax.ShapeDtypeStruct((nodes, widt...]
    all_to_all x1, waiting for transfers between devices: 4.68 us -> 6.94 us  [body(): lax.all_to_all(scorer, 'group', 0, 0, tiled=True).astype(F32)]
    pallas_call x1, Pallas kernels: 6.13 us -> 4.05 us  [call_layer(): pl.pallas_call(layer_kernel, out_shape=(jax.ShapeDtypeStruct((owners, 24,...]
  transfers between devices with their start and end apart: 3 -> 5, of which waited for: 3 -> 5; matrix products, arithmetic and copies ran while one was open for 2% -> 1% of each run, Pallas kernels for 4% -> 9%
where the time goes in v3:
time: 184 us; the launch traced here: 183 us
  waiting for transfers between devices  92.1 us (50%)
  Pallas kernels  36 us (20%)
  starting transfers between devices  35.7 us (19%)
  local copies, waits for them, and re-layouts  16.3 us (9%)
  other arithmetic  2.19 us (1%)
    all_to_all x1, waiting for transfers between devices, body(): fetched = near_core(lax.all_to_all(send, both, 0, 0, tiled=True))  40.3 us
    all_to_all x1, waiting for transfers between devices, body(): received = near_core(lax.all_to_all(out, both, 0, 0, tiled=True))  28 us
    pallas_call x1, Pallas kernels, call_slots(): pl.pallas_call(slots_kernel, out_shape=(jax.ShapeDtypeStruct((owners, 24,...  15.8 us
    all_to_all x1, starting transfers between devices, body(): fetched = near_core(lax.all_to_all(send, both, 0, 0, tiled=True))  14.4 us
    unnamed x56, local copies, waits for them, and re-layouts  13.9 us
    pallas_call x1, Pallas kernels, call_weights(): pl.pallas_call(weights_kernel, out_shape=(jax.ShapeDtypeStruct((8, 384, 1...  11.1 us
    all_to_all x1, waiting for transfers between devices, body(): lax.all_to_all(far, 'inner', 0, 0, tiled=True).astype(F32)  10.2 us
    all_to_all x1, starting transfers between devices, body(): received = near_core(lax.all_to_all(out, both, 0, 0, tiled=True))  7.43 us
  transfers between devices with their start and end apart: 5, of which 5 were waited for; matrix products, arithmetic and copies ran while one was open for 1% of the time, Pallas kernels for 9%

profile of v3, /device:TPU:32, one launch (start us, length us, event | category | flops | bytes accessed | tf_op | source)
XLA Modules:
  0.0 183.4 jit_solution(11753457799241330436)
XLA Ops:
  0.6 0.0 copy-start
  0.6 1.0 copy-done
  1.7 1.0 copy-done.2
  2.7 0.9 copy-done.11
  3.6 0.9 copy-done.13
  4.5 0.8 copy-done.18
  5.3 0.7 copy-done.24
  6.0 4.1 %layer.1 = (bf16[256,24,128]{2,1,0:T(8,128)(2,1)}, f32[1024,256]{1,0:T(8,128)S(1)}) custom-call(bf16[1024,256]{1,0:T(8,128)(2,1)S(1)} %copy-done, bf16[1024,256]{1,0:T(8,128)(2,1)S(1)} %copy-done.2, bf16[256,256]{1,0:T(8,128)(2,1)S(1)} %copy-done.11, bf16[256,256]{1,0:T(8,128)(2,1)S(1)} %copy-done.13, f32[1,256]{1,0:T(1,128)S(1)} %bitcast.52, ...), custom_call_target="tpu_custom_call" | custom-call | tf_op jit(solution)/shard_map/layer/pallas_call | solution.py:271
  10.1 1.0 copy-done.7
  11.1 14.4 %all-to-all-start = ((bf16[256,24,128]{2,1,0:T(8,128)(2,1)}), bf16[256,24,128]{2,1,0:T(8,128)(2,1)S(1)}, u32[]{:S(2)}, u32[]{:S(2)}) async-start(bf16[256,24,128]{2,1,0:T(8,128)(2,1)} %get-tuple-element.15), calls=%async_computation | async-start | bytes 3145728 | tf_op jit(solution)/shard_map/all_to_all | solution.py:378
  25.5 0.0 copy-start.9
  25.5 0.0 copy-start.21
  25.5 0.0 copy-start.22
  25.5 0.0 copy-start.23
  25.5 0.0 copy-done.20
  25.5 0.4 copy.54
  25.9 0.0 copy-done.25
  26.0 0.2 copy.51
  26.2 40.3 %all-to-all-done.chunks = bf16[256,24,128]{2,1,0:T(8,128)(2,1)S(1)} async-done(((bf16[256,24,128]{2,1,0:T(8,128)(2,1)}), bf16[256,24,128]{2,1,0:T(8,128)(2,1)S(1)}, u32[]{:S(2)}, u32[]{:S(2)}) %all-to-all-start) | async-done | bytes 1572896 | tf_op jit(solution)/shard_map/all_to_all | solution.py:378
  66.5 0.0 copy-done.9
  66.5 0.0 copy-done.21
  66.5 0.0 copy-done.22
  66.5 0.0 copy-done.23
  66.5 0.0 copy-start.4
  66.5 1.0 copy-done.4
  67.5 15.8 %slots.1 = (bf16[256,24,128]{2,1,0:T(8,128)(2,1)S(1)}, bf16[1024,256]{1,0:T(8,128)(2,1)S(1)}) custom-call(bf16[256,24,128]{2,1,0:T(8,128)(2,1)S(1)} %all-to-all-done.chunks, s32[1024,1]{1,0:T(8,128)S(1)} %bitcast.39, s32[1,1024]{1,0:T(1,128)S(1)} %bitcast.43, s32[2048,1]{1,0:T(8,128)S(1)} %bitcast.37, s32[4,512]{1,0:T(4,128)S(1)} %bitcast.45, ...), custom_call_target="tpu_custom_call" | custom-call | tf_op jit(solution)/shard_map/slots/pallas_call | solution.py:300
  83.3 0.0 copy-start.6
  83.3 1.2 copy-done.6
  84.5 0.8 copy-done.15
  85.3 7.4 %all-to-all-start.1 = ((bf16[256,24,128]{2,1,0:T(8,128)(2,1)}), bf16[256,24,128]{2,1,0:T(8,128)(2,1)S(1)}, u32[]{:S(2)}, u32[]{:S(2)}) async-start(bf16[256,24,128]{2,1,0:T(8,128)(2,1)} %copy-done.6), calls=%async_computation.1 | async-start | bytes 3145728 | tf_op jit(solution)/shard_map/all_to_all | solution.py:390
  92.8 0.0 copy-done.5
  92.8 0.0 copy-start.16
  92.8 1.0 copy-done.16
  93.8 11.1 %weights.1 = (bf16[8,384,128]{2,1,0:T(8,128)(2,1)S(1)}, f32[24,512]{1,0:T(8,128)S(1)}) custom-call(bf16[1024,256]{1,0:T(8,128)(2,1)S(1)} %copy-done.16, s32[2048,1]{1,0:T(8,128)S(1)} %bitcast.38, bf16[256,512]{1,0:T(8,128)(2,1)S(1)} %copy-done.9, f32[1,512]{1,0:T(1,128)S(1)} %bitcast.47, bf16[512,512]{1,0:T(8,128)(2,1)S(1)} %copy-done.5, ...), custom_call_target="tpu_custom_call" | custom-call | tf_op jit(solution)/shard_map/weights/pallas_call | solution.py:320
  104.9 0.0 copy-start.10
  104.9 0.9 copy-done.10
  105.8 28.0 %all-to-all-done.1.chunks = bf16[256,24,128]{2,1,0:T(8,128)(2,1)S(1)} async-done(((bf16[256,24,128]{2,1,0:T(8,128)(2,1)}), bf16[256,24,128]{2,1,0:T(8,128)(2,1)S(1)}, u32[]{:S(2)}, u32[]{:S(2)}) %all-to-all-start.1) | async-done | bytes 1572896 | tf_op jit(solution)/shard_map/all_to_all | solution.py:390
  133.8 4.2 %all-to-all-start.2 = ((bf16[8,384,128]{2,1,0:T(8,128)(2,1)}), bf16[8,384,128]{2,1,0:T(8,128)(2,1)}, u32[]{:S(2)}, u32[]{:S(2)}) async-start(bf16[8,384,128]{2,1,0:T(8,128)(2,1)} %copy-done.10), calls=%async_computation.2 | async-start | bytes 1572864 | tf_op jit(solution)/shard_map/all_to_all | solution.py:388
  138.0 0.0 copy-done.19
  138.0 0.1 copy.49
  138.1 0.1 slice.34
  138.3 0.1 reshape.76
  138.4 0.1 reshape.75
  138.5 0.0 copy-done.1
  138.5 0.0 copy-done.3
  138.5 0.0 copy-start.8
  138.5 1.2 copy-done.8
  139.7 3.7 %owner.1 = (bf16[1024,256]{1,0:T(8,128)(2,1)S(1)}, bf16[8,160,128]{2,1,0:T(8,128)(2,1)S(1)}) custom-call(bf16[256,24,128]{2,1,0:T(8,128)(2,1)S(1)} %all-to-all-done.1.chunks, s32[1,4096]{1,0:T(1,128)S(1)} %bitcast.41, f32[1024,256]{1,0:T(8,128)S(1)} %copy-done.8, bf16[1024,256]{1,0:T(8,128)(2,1)S(1)} %copy-done.1, bf16[1024,256]{1,0:T(8,128)(2,1)S(1)} %copy-done.3, ...), custom_call_target="tpu_custom_call" | custom-call | tf_op jit(solution)/shard_map/owner/pallas_call | solution.py:336
  143.5 0.0 copy-start.17
  143.5 0.7 copy-done.17
  144.2 6.9 %all-to-all-done.2 = bf16[8,384,128]{2,1,0:T(8,128)(2,1)} async-done(((bf16[8,384,128]{2,1,0:T(8,128)(2,1)}), bf16[8,384,128]{2,1,0:T(8,128)(2,1)}, u32[]{:S(2)}, u32[]{:S(2)}) %all-to-all-start.2) | async-done | bytes 786464 | tf_op jit(solution)/shard_map/all_to_all | solution.py:388
  151.1 3.4 %all-to-all-start.3 = ((bf16[8,160,128]{2,1,0:T(8,128)(2,1)}), bf16[8,160,128]{2,1,0:T(8,128)(2,1)S(1)}, u32[]{:S(2)}, u32[]{:S(2)}) async-start(bf16[8,160,128]{2,1,0:T(8,128)(2,1)} %copy-done.17), calls=%async_computation.3 | async-start | bytes 655360 | tf_op jit(solution)/shard_map/all_to_all | solution.py:399
  154.6 0.0 copy-start.12
  154.6 0.0 copy-start.14
  154.6 1.3 convert_reduce_fusion
  155.9 0.1 reshape.78
  156.0 6.7 %all-to-all-done.3 = bf16[8,160,128]{2,1,0:T(8,128)(2,1)S(1)} async-done(((bf16[8,160,128]{2,1,0:T(8,128)(2,1)}), bf16[8,160,128]{2,1,0:T(8,128)(2,1)S(1)}, u32[]{:S(2)}, u32[]{:S(2)}) %all-to-all-start.3) | async-done | bytes 327712 | tf_op jit(solution)/shard_map/all_to_all | solution.py:399
  162.8 0.8 pad_maximum_fusion
  163.6 6.3 %all-to-all-start.4 = ((bf16[32,32,128]{2,1,0:T(8,128)(2,1)}), bf16[32,32,128]{2,1,0:T(8,128)(2,1)S(1)}, u32[]{:S(2)}, u32[]{:S(2)}) async-start(bf16[32,32,128]{2,1,0:T(8,128)(2,1)} %pad_maximum_fusion), calls=%async_computation.4 | async-start | bytes 524288 | tf_op jit(solution)/shard_map/all_to_all | solution.py:409
  169.9 1.4 inputs.1
  171.4 10.2 %all-to-all-done.4 = bf16[32,32,128]{2,1,0:T(8,128)(2,1)S(1)} async-done(((bf16[32,32,128]{2,1,0:T(8,128)(2,1)}), bf16[32,32,128]{2,1,0:T(8,128)(2,1)S(1)}, u32[]{:S(2)}, u32[]{:S(2)}) %all-to-all-start.4) | async-done | bytes 262176 | tf_op jit(solution)/shard_map/all_to_all | solution.py:409
  181.6 0.6 slice_bitcast_fusion
  182.3 0.6 reshape.83
  182.9 0.6 copy.48
  (34 shorter events, 0.3 us)
Async XLA Ops:
  0.6 1.0 copy-start
  1.7 1.0 copy-start.2
  2.7 0.9 copy-start.11
  3.6 0.9 copy-start.13
  4.5 0.8 copy-start.18
  5.3 0.7 copy-start.24
  10.1 1.0 copy-start.7
  11.1 14.4 %copy-start.20 = (s32[512,4]{0,1:T(4,128)S(1)}, s32[512,4]{0,1:T(4,128)}, u32[]{:S(2)}) copy-start(s32[512,4]{0,1:T(4,128)} %param.25) | copy-start | bytes 24580
  11.1 14.8 %copy-start.25 = (s32[512,2]{0,1:T(2,128)S(1)}, s32[512,2]{0,1:T(2,128)}, u32[]{:S(2)}) copy-start(s32[512,2]{0,1:T(2,128)} %param.24) | copy-start | bytes 12292
  11.1 55.4 %all-to-all-start = ((bf16[256,24,128]{2,1,0:T(8,128)(2,1)}), bf16[256,24,128]{2,1,0:T(8,128)(2,1)S(1)}, u32[]{:S(2)}, u32[]{:S(2)}) async-start(bf16[256,24,128]{2,1,0:T(8,128)(2,1)} %get-tuple-element.15), calls=%async_computation | async-start | bytes 3145728 | tf_op jit(solution)/shard_map/all_to_all | solution.py:378
  25.5 41.0 %copy-start.9 = (bf16[256,512]{1,0:T(8,128)(2,1)S(1)}, bf16[256,512]{1,0:T(8,128)(2,1)}, u32[]{:S(2)}) copy-start(bf16[256,512]{1,0:T(8,128)(2,1)} %w1.3) | copy-start | bytes 786436
  25.5 41.0 %copy-start.21 = (f32[512]{0:T(512)S(1)}, f32[512]{0:T(512)}, u32[]{:S(2)}) copy-start(f32[512]{0:T(512)} %param.19) | copy-start | bytes 6148
  25.5 41.0 %copy-start.22 = (f32[512]{0:T(512)S(1)}, f32[512]{0:T(512)}, u32[]{:S(2)}) copy-start(f32[512]{0:T(512)} %param.21) | copy-start | bytes 6148
  25.5 41.0 %copy-start.23 = (f32[512]{0:T(512)S(1)}, f32[512]{0:T(512)}, u32[]{:S(2)}) copy-start(f32[512]{0:T(512)} %param.22) | copy-start | bytes 6148
  66.5 1.0 copy-start.4
  83.3 1.2 copy-start.6
  84.5 0.8 copy-start.15
  85.3 7.4 %copy-start.5 = (bf16[512,512]{1,0:T(8,128)(2,1)S(1)}, bf16[512,512]{1,0:T(8,128)(2,1)}, u32[]{:S(2)}) copy-start(bf16[512,512]{1,0:T(8,128)(2,1)} %w2.3) | copy-start | bytes 1572868
  85.3 48.5 %all-to-all-start.1 = ((bf16[256,24,128]{2,1,0:T(8,128)(2,1)}), bf16[256,24,128]{2,1,0:T(8,128)(2,1)S(1)}, u32[]{:S(2)}, u32[]{:S(2)}) async-start(bf16[256,24,128]{2,1,0:T(8,128)(2,1)} %copy-done.6), calls=%async_computation.1 | async-start | bytes 3145728 | tf_op jit(solution)/shard_map/all_to_all | solution.py:390
  92.8 1.0 copy-start.16
  93.8 44.2 %copy-start.19 = (s32[8,32,12]{1,0,2:T(8,128)S(1)}, s32[8,32,12]{1,0,2:T(8,128)}, u32[]{:S(2)}) copy-start(s32[8,32,12]{1,0,2:T(8,128)} %param.23) | copy-start | bytes 36868
  104.9 0.9 copy-start.10
  105.8 32.7 %copy-start.1 = (bf16[1024,256]{1,0:T(8,128)(2,1)S(1)}, bf16[1024,256]{1,0:T(8,128)(2,1)}, u32[]{:S(2)}) copy-start(bf16[1024,256]{1,0:T(8,128)(2,1)} %xs.3) | copy-start | bytes 1572868
  105.8 32.7 %copy-start.3 = (bf16[1024,256]{1,0:T(8,128)(2,1)S(1)}, bf16[1024,256]{1,0:T(8,128)(2,1)}, u32[]{:S(2)}) copy-start(bf16[1024,256]{1,0:T(8,128)(2,1)} %xa.3) | copy-start | bytes 1572868
  133.8 17.4 %all-to-all-start.2 = ((bf16[8,384,128]{2,1,0:T(8,128)(2,1)}), bf16[8,384,128]{2,1,0:T(8,128)(2,1)}, u32[]{:S(2)}, u32[]{:S(2)}) async-start(bf16[8,384,128]{2,1,0:T(8,128)(2,1)} %copy-done.10), calls=%async_computation.2 | async-start | bytes 1572864 | tf_op jit(solution)/shard_map/all_to_all | solution.py:388
  138.5 1.2 copy-start.8
  143.5 0.7 copy-start.17
  151.1 11.6 %all-to-all-start.3 = ((bf16[8,160,128]{2,1,0:T(8,128)(2,1)}), bf16[8,160,128]{2,1,0:T(8,128)(2,1)S(1)}, u32[]{:S(2)}, u32[]{:S(2)}) async-start(bf16[8,160,128]{2,1,0:T(8,128)(2,1)} %copy-done.17), calls=%async_computation.3 | async-start | bytes 655360 | tf_op jit(solution)/shard_map/all_to_all | solution.py:399
  154.6 15.3 %copy-start.12 = (bf16[256,256]{1,0:T(8,128)(2,1)S(1)}, bf16[256,256]{1,0:T(8,128)(2,1)}, u32[]{:S(2)}) copy-start(bf16[256,256]{1,0:T(8,128)(2,1)} %ws.3) | copy-start | bytes 393220
  154.6 15.3 %copy-start.14 = (bf16[256,256]{1,0:T(8,128)(2,1)S(1)}, bf16[256,256]{1,0:T(8,128)(2,1)}, u32[]{:S(2)}) copy-start(bf16[256,256]{1,0:T(8,128)(2,1)} %wn.3) | copy-start | bytes 393220
  163.6 17.9 %all-to-all-start.4 = ((bf16[32,32,128]{2,1,0:T(8,128)(2,1)}), bf16[32,32,128]{2,1,0:T(8,128)(2,1)S(1)}, u32[]{:S(2)}, u32[]{:S(2)}) async-start(bf16[32,32,128]{2,1,0:T(8,128)(2,1)} %pad_maximum_fusion), calls=%async_computation.4 | async-start | bytes 524288 | tf_op jit(solution)/shard_map/all_to_all | solution.py:409

commit v4 on v3

--- a/solution.py
+++ b/solution.py
@@ -9,6 +9,7 @@
 STEP = 32
 U2 = 4
 PARAMS = pltpu.CompilerParams(vmem_limit_bytes=36 * 1024 * 1024)
+WIDE = pltpu.CompilerParams(vmem_limit_bytes=60 * 1024 * 1024)
 F32 = jnp.float32
 BF16 = jnp.bfloat16
 
@@ -41,16 +42,34 @@
     return jnp.sum(jnp.where(lane == want, wide, 0.0), axis=1, keepdims=True)
 
 
-def layer_kernel(xs, xa, ws, wn, bl, lists, send, slope, tab):
+def layer_kernel(far_xs, far_xa, ws, wn, bl, lists, sent, far_slope, xs, xa, slope, tab, send, sems, loads, saves):
     nodes = xs.shape[0]
-    for r in range(nodes // 256):
+    steps = nodes // 256
+
+    def load(r, k):
         rows = pl.ds(r * 256, 256)
+        far, near = ((far_xs, xs), (far_xa, xa))[k]
+        return pltpu.make_async_copy(far.at[rows], near.at[rows], loads.at[k, r])
+
+    def save(r):
+        rows = pl.ds(r * 256, 256)
+        return pltpu.make_async_copy(slope.at[rows], far_slope.at[rows], saves.at[r])
+
+    for r in range(steps):
+        load(r, 0).start()
+        load(r, 1).start()
+    for r in range(steps):
+        rows = pl.ds(r * 256, 256)
+        load(r, 0).wait()
+        load(r, 1).wait()
         pre = dot(xs[rows, :], ws[...]) + dot(xa[rows, :], wn[...]) + bl[...]
         s = sigm(pre)
         t = pre * s
         tab[rows, :] = t.astype(BF16)
         slope[rows, :] = s + t * (1.0 - s)
+        save(r).start()
     owners = send.shape[0]
+    copies = []
     node_ids = lax.broadcasted_iota(jnp.int32, (256, nodes), 1).astype(F32)
 
     low = lax.broadcasted_iota(jnp.int32, (256, 128), 0) % 8 < 4
@@ -63,6 +82,12 @@
         y = dot(one_hot(column(mine, 8, 4), node_ids), tab[...])
         y = jnp.where(low, y[:, :128], y[:, 128:]).astype(BF16)
         send[at, 16:24, :] = y.reshape(32, 8, 128)
+        copies.append(pltpu.make_async_copy(send.at[pl.ds(b * 32, 32)], sent.at[pl.ds(b * 32, 32)], sems.at[b]))
+        copies[-1].start()
+    for copy in copies:
+        copy.wait()
+    for r in range(steps):
+        save(r).wait()
 
 
 def unpack(chunks, rows_ref):
@@ -153,13 +178,17 @@
 
 
 def slots_kernel(
-    chunks, pcol, plane, ncol, nlane, w1, b1, w2, b2, wo,
-    out, ends,
-    rows, grads, split, right, joint, h1, sl1, a1, a2, d1, d2,
+    chunks, pcol, plane, ncol, nlane, far_w1, b1, far_w2, b2, wo,
+    sent, far_ends,
+    rows, grads, split, out, sems, ends, w1, w2, others, right, joint, h1, sl1, a1, a2, d1, d2,
 ):
     owners = chunks.shape[0]
     table = owners * 16
     pos = ends.shape[0] // 2
+    load_w1 = pltpu.make_async_copy(far_w1, w1, others.at[0])
+    load_w2 = pltpu.make_async_copy(far_w2, w2, others.at[1])
+    load_w1.start()
+    load_w2.start()
     unpack(chunks, rows)
     slot_ids = lax.broadcasted_iota(jnp.int32, (256, table), 1)
 
@@ -169,6 +198,10 @@
         return carry
 
     lax.fori_loop(0, 2 * pos // 256, fetch, 0, unroll=U2)
+    save_ends = pltpu.make_async_copy(ends, far_ends, others.at[2])
+    save_ends.start()
+    load_w1.wait()
+    load_w2.wait()
     grads[...] = jnp.zeros_like(grads)
     pair_blocks(
         ends, right, joint, h1, sl1, a1, a2, d1, d2, ncol, nlane, w1, b1, w2, b2, wo, grads, None, None, None
@@ -180,22 +213,21 @@
     def spread(ids):
         return dot(one_hot(plane[...], ids), split[...])
 
-    def full(b, carry):
+    low = lax.broadcasted_iota(jnp.int32, (256, 128), 0) % 8 < 4
+    copies = []
+    for b in range(owners // 32):
+        at = slice(b * 32, b * 32 + 32)
         y = spread(sub + b * 256).astype(BF16)
-        out[pl.ds(b * 32, 32), 0:8, :] = y[:, :128].reshape(32, 8, 128)
-        out[pl.ds(b * 32, 32), 8:16, :] = y[:, 128:].reshape(32, 8, 128)
-        return carry
-
-    lax.fori_loop(0, owners // 32, full, 0, unroll=U2)
-    low = lax.broadcasted_iota(jnp.int32, (256, 128), 0) % 8 < 4
-
-    def mixed(b, carry):
+        out[at, 0:8, :] = y[:, :128].reshape(32, 8, 128)
+        out[at, 8:16, :] = y[:, 128:].reshape(32, 8, 128)
         y = spread(sub_mixed + (owners * 8 + b * 256))
         y = jnp.where(low, y[:, :128], y[:, 128:]).astype(BF16)
-        out[pl.ds(b * 32, 32), 16:24, :] = y.reshape(32, 8, 128)
-        return carry
-
-    lax.fori_loop(0, owners // 32, mixed, 0, unroll=U2)
+        out[at, 16:24, :] = y.reshape(32, 8, 128)
+        copies.append(pltpu.make_async_copy(out.at[pl.ds(b * 32, 32)], sent.at[pl.ds(b * 32, 32)], sems.at[b]))
+        copies[-1].start()
+    for copy in copies:
+        copy.wait()
+    save_ends.wait()
 
 
 def weights_kernel(
@@ -223,13 +255,16 @@
 
 
 def owner_kernel(
-    chunks, lanes, slope, xs, xa, bias,
+    chunks, lanes, far_slope, xs, xa, bias,
     dpre, terms,
-    rows, sums,
+    rows, sums, slope, sem,
 ):
     table = lanes.shape[1]
     nodes = xs.shape[0]
+    load = pltpu.make_async_copy(far_slope, slope, sem.at[0])
+    load.start()
     unpack(chunks, rows)
+    load.wait()
     ids = lax.broadcasted_iota(jnp.int32, (256, table), 0)
 
     def nodes_step(b, carry):
@@ -271,11 +306,22 @@
     return pl.pallas_call(
         layer_kernel,
         out_shape=(
-            jax.ShapeDtypeStruct((owners, 24, 128), BF16),
-            jax.ShapeDtypeStruct((nodes, width), F32),
+            pltpu.HBM((owners, 24, 128), BF16),
+            pltpu.HBM((nodes, width), F32),
         ),
-        scratch_shapes=[pltpu.VMEM((nodes, width), BF16)],
-        compiler_params=PARAMS,
+        in_specs=[pl.BlockSpec(memory_space=pltpu.HBM)] * 2 + [pl.BlockSpec(memory_space=pltpu.VMEM)] * 4,
+        out_specs=(pl.BlockSpec(memory_space=pltpu.HBM), pl.BlockSpec(memory_space=pltpu.HBM)),
+        scratch_shapes=[
+            pltpu.VMEM((nodes, width), BF16),
+            pltpu.VMEM((nodes, width), BF16),
+            pltpu.VMEM((nodes, width), F32),
+            pltpu.VMEM((nodes, width), BF16),
+            pltpu.VMEM((owners, 24, 128), BF16),
+            pltpu.SemaphoreType.DMA((owners // 32,)),
+            pltpu.SemaphoreType.DMA((2, nodes // 256)),
+            pltpu.SemaphoreType.DMA((nodes // 256,)),
+        ],
+        compiler_params=WIDE,
         name="layer",
     )(*args)
 
@@ -300,13 +346,21 @@
     return pl.pallas_call(
         slots_kernel,
         out_shape=(
-            jax.ShapeDtypeStruct((owners, 24, 128), BF16),
-            jax.ShapeDtypeStruct((2 * pos, width), BF16),
+            pltpu.HBM((owners, 24, 128), BF16),
+            pltpu.HBM((2 * pos, width), BF16),
         ),
+        in_specs=[pl.BlockSpec(memory_space=pltpu.HBM if k in (5, 7) else pltpu.VMEM) for k in range(10)],
+        out_specs=(pl.BlockSpec(memory_space=pltpu.HBM), pl.BlockSpec(memory_space=pltpu.HBM)),
         scratch_shapes=[
             pltpu.VMEM((owners * 16, width), BF16),
             pltpu.VMEM((2 * pos, width), F32),
             pltpu.VMEM((2 * pos, width), BF16),
+            pltpu.VMEM((owners, 24, 128), BF16),
+            pltpu.SemaphoreType.DMA((owners // 32,)),
+            pltpu.VMEM((2 * pos, width), BF16),
+            pltpu.VMEM((width, hidden), BF16),
+            pltpu.VMEM((hidden, hidden), BF16),
+            pltpu.SemaphoreType.DMA((3,)),
         ]
         + block_scratch(pos, width, hidden),
         compiler_params=PARAMS,
@@ -337,9 +391,15 @@
         owner_kernel,
         out_shape=(
             jax.ShapeDtypeStruct((nodes, width), BF16),
-            jax.ShapeDtypeStruct((8, 160, 128), BF16),
+            pltpu.HBM((8, 160, 128), BF16),
         ),
-        scratch_shapes=[pltpu.VMEM((table, width), BF16), pltpu.VMEM((16, 128), F32)],
+        in_specs=[pl.BlockSpec(memory_space=pltpu.HBM if k == 2 else pltpu.VMEM) for k in range(6)],
+        scratch_shapes=[
+            pltpu.VMEM((table, width), BF16),
+            pltpu.VMEM((16, 128), F32),
+            pltpu.VMEM((nodes, width), F32),
+            pltpu.SemaphoreType.DMA((1,)),
+        ],
         compiler_params=PARAMS,
         name="owner",
     )(*args)
@@ -357,6 +417,10 @@
     )(*args)
 
 
+def far_core(x):
+    return pltpu.with_memory_space_constraint(x, pltpu.HBM)
+
+
 def near_core(x):
     return pltpu.with_memory_space_constraint(x, pltpu.VMEM)
 
@@ -365,16 +429,15 @@
     x_self, x_agg, w_self, w_nbr, b_layer, w_one, b_one, w_two, b_two, w_out,
     send_lists, endpoint_slots, neg_index,
 ):
-    nodes, width = x_self.shape
     both = ("group", "inner")
     owners = lax.axis_size("group") * lax.axis_size("inner")
     pos = endpoint_slots.shape[0]
     negs = neg_index.shape[1]
-    hidden = w_one.shape[1]
     pairs = pos * (1 + negs)
     table = owners * 16
     lists = send_lists.reshape(owners, 12)
-    send, slope = call_layer(x_self, x_agg, w_self, w_nbr, b_layer.reshape(1, -1), send_lists.transpose(2, 0, 1))
+    send, slope = call_layer(far_core(x_self), far_core(x_agg), w_self, w_nbr, b_layer.reshape(1, -1), send_lists.transpose(2, 0, 1))
+    w_one_far, w_two_far = far_core(w_one), far_core(w_two)
     fetched = near_core(lax.all_to_all(send, both, 0, 0, tiled=True))
     owner = endpoint_slots // 12
     column = endpoint_slots - owner * 12
@@ -383,9 +446,16 @@
     neg_t = neg_index.T
     ncol = neg_t.reshape(-1, 1)
     scorer_args = (w_one, b_one.reshape(1, -1), w_two, b_two.reshape(1, -1), w_out.reshape(1, -1))
-    out, ends = call_slots(fetched, place.reshape(-1, 1), place.reshape(1, -1), ncol, neg_t, *scorer_args)
+    out, ends = call_slots(fetched, place.reshape(-1, 1), place.reshape(1, -1), ncol, neg_t, w_one_far, scorer_args[1], w_two_far, *scorer_args[3:])
     scorer, bias = call_weights(ends, ncol, *scorer_args)
-    first = jnp.sum(lax.all_to_all(scorer, "group", 0, 0, tiled=True).astype(F32), axis=0)
+    groups = lax.axis_size("group")
+    here = lax.axis_index("group")
+    pieces = [lax.dynamic_index_in_dim(scorer, here, 0, False).astype(F32)]
+    for k in range(1, groups):
+        piece = lax.dynamic_index_in_dim(scorer, (here + k) % groups, 0, False)
+        moves = [(g, (g + k) % groups) for g in range(groups)]
+        pieces.append(lax.ppermute(piece, "group", moves).astype(F32))
+    first = sum(pieces)
     first = lax.optimization_barrier(first)
     received = near_core(lax.all_to_all(out, both, 0, 0, tiled=True))
     lanes = jnp.concatenate(
@@ -394,7 +464,7 @@
             jnp.pad(lists[:, 8:], ((0, 0), (0, 4)), constant_values=-1).reshape(-1),
         ]
     ).reshape(1, table)
-    d_pre, terms = call_owner(received, lanes, slope, x_self, x_agg, bias)
+    d_pre, terms = call_owner(received, lanes, far_core(slope), x_self, x_agg, bias)
     grad_self, grad_agg = call_inputs(d_pre, w_self, w_nbr)
     near = jnp.sum(lax.all_to_all(terms, "group", 0, 0, tiled=True).astype(F32), axis=0)
     sums = near[128:144] + near[144:160]

time: 184 us -> 165 us (0.90)
  waiting for transfers between devices: 92.1 us -> 77.7 us
  local copies, waits for them, and re-layouts: 16.3 us -> 5.76 us
  Pallas kernels: 36 us -> 40.1 us
  starting transfers between devices: 35.7 us -> 37.6 us
    all_to_all x1, waiting for transfers between devices: 28 us -> 9.42 us  [body(): received = near_core(lax.all_to_all(out, both, 0, 0, tiled=True))]
    unnamed x56 -> x36, local copies, waits for them, and re-layouts: 13.9 us -> 2.56 us
    ppermute x0 -> x7, waiting for transfers between devices: none -> 11.1 us  [body(): pieces.append(lax.ppermute(piece, 'group', moves).astype(F32))]
    all_to_all x1 -> x0, waiting for transfers between devices: 6.94 us -> none  [body(): lax.all_to_all(scorer, 'group', 0, 0, tiled=True).astype(F32)]
    ppermute x0 -> x7, starting transfers between devices: none -> 6.19 us  [body(): pieces.append(lax.ppermute(piece, 'group', moves).astype(F32))]
    all_to_all x1 -> x0, starting transfers between devices: 4.21 us -> none  [body(): lax.all_to_all(scorer, 'group', 0, 0, tiled=True).astype(F32)]
    pallas_call x2, Pallas kernels: 19.8 us -> 22.3 us  [the longest x1 16 us: call_slots(): pl.pallas_call(slots_kernel, out_shape=(pltpu.HBM((owners, 24, 128), BF16...]
  transfers between devices with their start and end apart: 5 -> 11, of which waited for: 5 -> 6; matrix products, arithmetic and copies ran while one was open for 1% -> 2% of each run, Pallas kernels for 9% -> 11%
where the time goes in v4:
time: 165 us
  waiting for transfers between devices  77.7 us (47%)
  Pallas kernels  40.1 us (24%)
  starting transfers between devices  37.6 us (23%)
  local copies, waits for them, and re-layouts  5.76 us (3%)
  other arithmetic  2.24 us (1%)
    all_to_all x1, waiting for transfers between devices, body(): fetched = near_core(lax.all_to_all(send, both, 0, 0, tiled=True))  40.3 us
    pallas_call x1, Pallas kernels, call_slots(): pl.pallas_call(slots_kernel, out_shape=(pltpu.HBM((owners, 24, 128), BF16...  16 us
    all_to_all x1, starting transfers between devices, body(): fetched = near_core(lax.all_to_all(send, both, 0, 0, tiled=True))  14.4 us
    ppermute x7, waiting for transfers between devices, body(): pieces.append(lax.ppermute(piece, 'group', moves).astype(F32))  11.1 us
    pallas_call x1, Pallas kernels, call_weights(): pl.pallas_call(weights_kernel, out_shape=(jax.ShapeDtypeStruct((8, 384, 1...  11 us
    all_to_all x1, waiting for transfers between devices, body(): lax.all_to_all(far, 'inner', 0, 0, tiled=True).astype(F32)  10.2 us
    all_to_all x1, waiting for transfers between devices, body(): received = near_core(lax.all_to_all(out, both, 0, 0, tiled=True))  9.42 us
    all_to_all x1, starting transfers between devices, body(): received = near_core(lax.all_to_all(out, both, 0, 0, tiled=True))  7.44 us
  transfers between devices with their start and end apart: 11, of which 6 were waited for; matrix products, arithmetic and copies ran while one was open for 2% of the time, Pallas kernels for 11%

profile of v4, /device:TPU:32, one launch (start us, length us, event | category | flops | bytes accessed | tf_op | source)
XLA Modules:
  0.0 164.5 jit_solution(12013153062546472258)
XLA Ops:
  0.6 6.2 %layer.1 = (bf16[256,24,128]{2,1,0:T(8,128)(2,1)}, f32[1024,256]{1,0:T(8,128)}) custom-call(bf16[1024,256]{1,0:T(8,128)(2,1)} %xs.1, bf16[1024,256]{1,0:T(8,128)(2,1)} %xa.1, bf16[256,256]{1,0:T(8,128)(2,1)} %ws.3, bf16[256,256]{1,0:T(8,128)(2,1)} %wn.3, f32[1,256]{1,0:T(1,128)} %bitcast.79, s32[12,8,32]{2,1,0:T(8,128)} %bitcast.72), custom_call_target="tpu_custom_call" | custom-call | tf_op jit(solution)/shard_map/layer/pallas_call | solution.py:306
  6.9 0.0 copy-start.15
  6.9 0.0 copy-start.8
  6.9 14.4 %all-to-all-start = ((bf16[256,24,128]{2,1,0:T(8,128)(2,1)}), bf16[256,24,128]{2,1,0:T(8,128)(2,1)S(1)}, u32[]{:S(2)}, u32[]{:S(2)}) async-start(bf16[256,24,128]{2,1,0:T(8,128)(2,1)} %get-tuple-element.15), calls=%async_computation | async-start | bytes 3145728 | tf_op jit(solution)/shard_map/all_to_all | solution.py:441
  21.3 0.0 copy-done.15
  21.3 0.0 copy-start.9
  21.3 0.0 copy-start.10
  21.3 0.0 copy-start.11
  21.4 0.2 copy.51
  21.6 0.0 copy-done.8
  21.6 0.4 copy.54
  22.0 40.3 %all-to-all-done.chunks = bf16[256,24,128]{2,1,0:T(8,128)(2,1)S(1)} async-done(((bf16[256,24,128]{2,1,0:T(8,128)(2,1)}), bf16[256,24,128]{2,1,0:T(8,128)(2,1)S(1)}, u32[]{:S(2)}, u32[]{:S(2)}) %all-to-all-start) | async-done | bytes 1572896 | tf_op jit(solution)/shard_map/all_to_all | solution.py:441
  62.3 0.0 copy-done.9
  62.3 0.0 copy-done.10
  62.3 0.0 copy-done.11
  62.3 16.0 %slots.1 = (bf16[256,24,128]{2,1,0:T(8,128)(2,1)}, bf16[1024,256]{1,0:T(8,128)(2,1)}) custom-call(bf16[256,24,128]{2,1,0:T(8,128)(2,1)S(1)} %all-to-all-done.chunks, s32[1024,1]{1,0:T(8,128)S(1)} %bitcast.56, s32[1,1024]{1,0:T(1,128)S(1)} %bitcast.59, s32[2048,1]{1,0:T(8,128)S(1)} %bitcast.54, s32[4,512]{1,0:T(4,128)S(1)} %bitcast.61, bf16[256,512]{1,0:T(8,128)(2,1)} %w1.1, ...), custom_call_target="tpu_custom_call" | custom-call | tf_op jit(solution)/shard_map/slots/pallas_call | solution.py:346
  78.4 0.0 copy-start.2
  78.4 0.0 copy-start.3
  78.4 7.4 %all-to-all-start.1 = ((bf16[256,24,128]{2,1,0:T(8,128)(2,1)}), bf16[256,24,128]{2,1,0:T(8,128)(2,1)S(1)}, u32[]{:S(2)}, u32[]{:S(2)}) async-start(bf16[256,24,128]{2,1,0:T(8,128)(2,1)} %get-tuple-element.16), calls=%async_computation.1 | async-start | bytes 3145728 | tf_op jit(solution)/shard_map/all_to_all | solution.py:460
  85.9 0.0 copy-done.2
  85.9 0.0 copy-done.3
  86.0 0.0 copy-start.7
  86.0 1.0 copy-done.7
  87.0 11.0 %weights.1 = (bf16[8,384,128]{2,1,0:T(8,128)(2,1)S(1)}, f32[24,512]{1,0:T(8,128)S(1)}) custom-call(bf16[1024,256]{1,0:T(8,128)(2,1)S(1)} %copy-done.7, s32[2048,1]{1,0:T(8,128)S(1)} %bitcast.55, bf16[256,512]{1,0:T(8,128)(2,1)S(1)} %copy-done.3, f32[1,512]{1,0:T(1,128)S(1)} %bitcast.63, bf16[512,512]{1,0:T(8,128)(2,1)S(1)} %copy-done.2, ...), custom_call_target="tpu_custom_call" | custom-call | tf_op jit(solution)/shard_map/weights/pallas_call | solution.py:374
  98.1 0.0 copy-start.4
  98.1 0.0 copy-start
  98.1 0.0 copy-start.1
  98.1 0.8 copy-done.4
  98.9 0.8 dynamic-slice_bitcast_fusion.6
  99.7 2.5 %collective-permute-start.6 = (bf16[384,128]{1,0:T(8,128)(2,1)}, bf16[384,128]{1,0:T(8,128)(2,1)S(1)}, u32[]{:S(2)}, u32[]{:S(2)}) collective-permute-start(bf16[384,128]{1,0:T(8,128)(2,1)} %get-tuple-element.26), channel_id=1, source_target_pairs={{0,224},{32,0},{64,32},{96,64},{128,96},{160,128},{192,160},{224,1... | collective-permute-start | bytes 294920 | tf_op jit(solution)/shard_map/ppermute | solution.py:457
  102.2 0.8 collective-permute-start.5
  103.0 0.0 copy-done.12
  103.0 0.1 copy.49
  103.1 0.1 slice.34
  103.3 0.1 reshape.78
  103.4 0.1 reshape.77
  103.5 0.2 collective-permute-start.4
  103.6 2.7 %collective-permute-start.3 = (bf16[384,128]{1,0:T(8,128)(2,1)}, bf16[384,128]{1,0:T(8,128)(2,1)}, u32[]{:S(2)}, u32[]{:S(2)}) collective-permute-start(bf16[384,128]{1,0:T(8,128)(2,1)} %get-tuple-element.29), channel_id=1, source_target_pairs={{0,128},{32,160},{64,192},{96,224},{128,0},{160,32},{192,64},{224,... | collective-permute-start | bytes 294920 | tf_op jit(solution)/shard_map/ppermute | solution.py:457
  106.3 0.0 collective-permute-start.2
  106.4 0.7 collective-permute-done.6
  107.0 0.0 collective-permute-start.1
  107.0 10.5 %collective-permute-done.5 = bf16[384,128]{1,0:T(8,128)(2,1)} collective-permute-done((bf16[384,128]{1,0:T(8,128)(2,1)}, bf16[384,128]{1,0:T(8,128)(2,1)}, u32[]{:S(2)}, u32[]{:S(2)}) %collective-permute-start.5) | collective-permute-done | bytes 98336 | tf_op jit(solution)/shard_map/ppermute | solution.py:457
  117.5 0.0 collective-permute-start
  117.5 9.4 %all-to-all-done.1.chunks = bf16[256,24,128]{2,1,0:T(8,128)(2,1)S(1)} async-done(((bf16[256,24,128]{2,1,0:T(8,128)(2,1)}), bf16[256,24,128]{2,1,0:T(8,128)(2,1)S(1)}, u32[]{:S(2)}, u32[]{:S(2)}) %all-to-all-start.1) | async-done | bytes 1572896 | tf_op jit(solution)/shard_map/all_to_all | solution.py:460
  126.9 0.0 copy-done.13
  126.9 0.0 copy-done.1
  126.9 5.3 %owner.1 = (bf16[1024,256]{1,0:T(8,128)(2,1)S(1)}, bf16[8,160,128]{2,1,0:T(8,128)(2,1)}) custom-call(bf16[256,24,128]{2,1,0:T(8,128)(2,1)S(1)} %all-to-all-done.1.chunks, s32[1,4096]{1,0:T(1,128)S(1)} %bitcast.57, f32[1024,256]{1,0:T(8,128)} %get-tuple-element.17.far_slope, bf16[1024,256]{1,0:T(8,128)(2,1)S(1)} %copy-done, bf16[1024,256]{1,0:T(8,128)(2,1)S(1)} %copy-done.1, ...), custom_call_target="tpu_custom_call" | custom-call | tf_op jit(solution)/shard_map/owner/pallas_call | solution.py:390
  132.3 3.5 %all-to-all-start.2 = ((bf16[8,160,128]{2,1,0:T(8,128)(2,1)}), bf16[8,160,128]{2,1,0:T(8,128)(2,1)S(1)}, u32[]{:S(2)}, u32[]{:S(2)}) async-start(bf16[8,160,128]{2,1,0:T(8,128)(2,1)} %get-tuple-element.24), calls=%async_computation.2 | async-start | bytes 655360 | tf_op jit(solution)/shard_map/all_to_all | solution.py:469
  135.8 0.0 copy-start.6
  135.8 0.0 collective-permute-done.4
  135.8 0.0 collective-permute-done.3
  135.8 0.0 collective-permute-done.2
  135.8 0.0 collective-permute-done.1
  135.8 0.0 collective-permute-done
  135.9 1.3 fusion.5
  137.2 0.1 reshape.80
  137.3 6.7 %all-to-all-done.2 = bf16[8,160,128]{2,1,0:T(8,128)(2,1)S(1)} async-done(((bf16[8,160,128]{2,1,0:T(8,128)(2,1)}), bf16[8,160,128]{2,1,0:T(8,128)(2,1)S(1)}, u32[]{:S(2)}, u32[]{:S(2)}) %all-to-all-start.2) | async-done | bytes 327712 | tf_op jit(solution)/shard_map/all_to_all | solution.py:469
  144.1 0.8 pad_maximum_fusion
  144.9 6.1 %all-to-all-start.3 = ((bf16[32,32,128]{2,1,0:T(8,128)(2,1)}), bf16[32,32,128]{2,1,0:T(8,128)(2,1)S(1)}, u32[]{:S(2)}, u32[]{:S(2)}) async-start(bf16[32,32,128]{2,1,0:T(8,128)(2,1)} %pad_maximum_fusion), calls=%async_computation.3 | async-start | bytes 524288 | tf_op jit(solution)/shard_map/all_to_all | solution.py:479
  151.0 1.4 inputs.1
  152.5 10.2 %all-to-all-done.3 = bf16[32,32,128]{2,1,0:T(8,128)(2,1)S(1)} async-done(((bf16[32,32,128]{2,1,0:T(8,128)(2,1)}), bf16[32,32,128]{2,1,0:T(8,128)(2,1)S(1)}, u32[]{:S(2)}, u32[]{:S(2)}) %all-to-all-start.3) | async-done | bytes 262176 | tf_op jit(solution)/shard_map/all_to_all | solution.py:479
  162.7 0.6 slice_bitcast_fusion
  163.3 0.6 reshape.85
  164.0 0.6 copy.48
  (27 shorter events, 0.3 us)
Async XLA Ops:
  6.9 14.4 %copy-start.15 = (s32[512,2]{0,1:T(2,128)S(1)}, s32[512,2]{0,1:T(2,128)}, u32[]{:S(2)}) copy-start(s32[512,2]{0,1:T(2,128)} %param.24) | copy-start | bytes 12292
  6.9 14.7 %copy-start.8 = (s32[512,4]{0,1:T(4,128)S(1)}, s32[512,4]{0,1:T(4,128)}, u32[]{:S(2)}) copy-start(s32[512,4]{0,1:T(4,128)} %param.25) | copy-start | bytes 24580
  6.9 55.4 %all-to-all-start = ((bf16[256,24,128]{2,1,0:T(8,128)(2,1)}), bf16[256,24,128]{2,1,0:T(8,128)(2,1)S(1)}, u32[]{:S(2)}, u32[]{:S(2)}) async-start(bf16[256,24,128]{2,1,0:T(8,128)(2,1)} %get-tuple-element.15), calls=%async_computation | async-start | bytes 3145728 | tf_op jit(solution)/shard_map/all_to_all | solution.py:441
  21.3 41.0 %copy-start.9 = (f32[512]{0:T(512)S(1)}, f32[512]{0:T(512)}, u32[]{:S(2)}) copy-start(f32[512]{0:T(512)} %param.19) | copy-start | bytes 6148
  21.3 41.0 %copy-start.10 = (f32[512]{0:T(512)S(1)}, f32[512]{0:T(512)}, u32[]{:S(2)}) copy-start(f32[512]{0:T(512)} %param.21) | copy-start | bytes 6148
  21.3 41.0 %copy-start.11 = (f32[512]{0:T(512)S(1)}, f32[512]{0:T(512)}, u32[]{:S(2)}) copy-start(f32[512]{0:T(512)} %param.22) | copy-start | bytes 6148
  78.4 7.6 %copy-start.2 = (bf16[512,512]{1,0:T(8,128)(2,1)S(1)}, bf16[512,512]{1,0:T(8,128)(2,1)}, u32[]{:S(2)}) copy-start(bf16[512,512]{1,0:T(8,128)(2,1)} %w2.1) | copy-start | bytes 1572868
  78.4 7.6 %copy-start.3 = (bf16[256,512]{1,0:T(8,128)(2,1)S(1)}, bf16[256,512]{1,0:T(8,128)(2,1)}, u32[]{:S(2)}) copy-start(bf16[256,512]{1,0:T(8,128)(2,1)} %w1.1) | copy-start | bytes 786436
  78.4 48.5 %all-to-all-start.1 = ((bf16[256,24,128]{2,1,0:T(8,128)(2,1)}), bf16[256,24,128]{2,1,0:T(8,128)(2,1)S(1)}, u32[]{:S(2)}, u32[]{:S(2)}) async-start(bf16[256,24,128]{2,1,0:T(8,128)(2,1)} %get-tuple-element.16), calls=%async_computation.1 | async-start | bytes 3145728 | tf_op jit(solution)/shard_map/all_to_all | solution.py:460
  86.0 1.0 copy-start.7
  87.0 16.0 %copy-start.12 = (s32[8,32,12]{1,0,2:T(8,128)S(1)}, s32[8,32,12]{1,0,2:T(8,128)}, u32[]{:S(2)}) copy-start(s32[8,32,12]{1,0,2:T(8,128)} %param.23) | copy-start | bytes 36868
  98.1 0.9 copy-start.4
  98.1 28.9 %copy-start = (bf16[1024,256]{1,0:T(8,128)(2,1)S(1)}, bf16[1024,256]{1,0:T(8,128)(2,1)}, u32[]{:S(2)}) copy-start(bf16[1024,256]{1,0:T(8,128)(2,1)} %xs.1) | copy-start | bytes 1572868
  98.1 28.9 %copy-start.1 = (bf16[1024,256]{1,0:T(8,128)(2,1)S(1)}, bf16[1024,256]{1,0:T(8,128)(2,1)}, u32[]{:S(2)}) copy-start(bf16[1024,256]{1,0:T(8,128)(2,1)} %xa.1) | copy-start | bytes 1572868
  99.7 7.3 %collective-permute-start.6 = (bf16[384,128]{1,0:T(8,128)(2,1)}, bf16[384,128]{1,0:T(8,128)(2,1)S(1)}, u32[]{:S(2)}, u32[]{:S(2)}) collective-permute-start(bf16[384,128]{1,0:T(8,128)(2,1)} %get-tuple-element.26), channel_id=1, source_target_pairs={{0,224},{32,0},{64,32},{96,64},{128,96},{160,128},{192,160},{224,1... | collective-permute-start | bytes 294920 | tf_op jit(solution)/shard_map/ppermute | solution.py:457
  102.2 15.3 %collective-permute-start.5 = (bf16[384,128]{1,0:T(8,128)(2,1)}, bf16[384,128]{1,0:T(8,128)(2,1)}, u32[]{:S(2)}, u32[]{:S(2)}) collective-permute-start(bf16[384,128]{1,0:T(8,128)(2,1)} %get-tuple-element.27), channel_id=1, source_target_pairs={{0,192},{32,224},{64,0},{96,32},{128,64},{160,96},{192,128},{224,1... | collective-permute-start | bytes 294920 | tf_op jit(solution)/shard_map/ppermute | solution.py:457
  103.5 32.3 %collective-permute-start.4 = (bf16[384,128]{1,0:T(8,128)(2,1)}, bf16[384,128]{1,0:T(8,128)(2,1)}, u32[]{:S(2)}, u32[]{:S(2)}) collective-permute-start(bf16[384,128]{1,0:T(8,128)(2,1)} %get-tuple-element.28), channel_id=1, source_target_pairs={{0,160},{32,192},{64,224},{96,0},{128,32},{160,64},{192,96},{224,1... | collective-permute-start | bytes 294920 | tf_op jit(solution)/shard_map/ppermute | solution.py:457
  103.6 32.2 %collective-permute-start.3 = (bf16[384,128]{1,0:T(8,128)(2,1)}, bf16[384,128]{1,0:T(8,128)(2,1)}, u32[]{:S(2)}, u32[]{:S(2)}) collective-permute-start(bf16[384,128]{1,0:T(8,128)(2,1)} %get-tuple-element.29), channel_id=1, source_target_pairs={{0,128},{32,160},{64,192},{96,224},{128,0},{160,32},{192,64},{224,... | collective-permute-start | bytes 294920 | tf_op jit(solution)/shard_map/ppermute | solution.py:457
  106.3 29.5 %collective-permute-start.2 = (bf16[384,128]{1,0:T(8,128)(2,1)}, bf16[384,128]{1,0:T(8,128)(2,1)}, u32[]{:S(2)}, u32[]{:S(2)}) collective-permute-start(bf16[384,128]{1,0:T(8,128)(2,1)} %get-tuple-element.30), channel_id=1, source_target_pairs={{0,96},{32,128},{64,160},{96,192},{128,224},{160,0},{192,32},{224,... | collective-permute-start | bytes 294920 | tf_op jit(solution)/shard_map/ppermute | solution.py:457
  107.0 19.9 %copy-start.13 = (bf16[384,128]{1,0:T(8,128)(2,1)}, bf16[384,128]{1,0:T(8,128)(2,1)S(1)}, u32[]{:S(2)}) copy-start(bf16[384,128]{1,0:T(8,128)(2,1)S(1)} %collective-permute-done.6) | copy-start | bytes 294916
  107.0 28.8 %collective-permute-start.1 = (bf16[384,128]{1,0:T(8,128)(2,1)S(1)}, bf16[384,128]{1,0:T(8,128)(2,1)}, u32[]{:S(2)}, u32[]{:S(2)}) collective-permute-start(bf16[384,128]{1,0:T(8,128)(2,1)S(1)} %get-tuple-element.31), channel_id=1, source_target_pairs={{0,64},{32,96},{64,128},{96,160},{128,192},{160,224},{192,0},{224,... | collective-permute-start | bytes 294920 | tf_op jit(solution)/shard_map/ppermute | solution.py:457
  117.5 18.3 %collective-permute-start = (bf16[384,128]{1,0:T(8,128)(2,1)S(1)}, bf16[384,128]{1,0:T(8,128)(2,1)}, u32[]{:S(2)}, u32[]{:S(2)}) collective-permute-start(bf16[384,128]{1,0:T(8,128)(2,1)S(1)} %get-tuple-element.25), channel_id=1, source_target_pairs={{0,32},{32,64},{64,96},{96,128},{128,160},{160,192},{192,224},{224... | collective-permute-start | bytes 294920 | tf_op jit(solution)/shard_map/ppermute | solution.py:457
  126.9 8.9 %copy-start.14 = (bf16[384,128]{1,0:T(8,128)(2,1)S(1)}, bf16[384,128]{1,0:T(8,128)(2,1)}, u32[]{:S(2)}) copy-start(bf16[384,128]{1,0:T(8,128)(2,1)} %copy-done.13) | copy-start | bytes 294916
  132.3 11.7 %all-to-all-start.2 = ((bf16[8,160,128]{2,1,0:T(8,128)(2,1)}), bf16[8,160,128]{2,1,0:T(8,128)(2,1)S(1)}, u32[]{:S(2)}, u32[]{:S(2)}) async-start(bf16[8,160,128]{2,1,0:T(8,128)(2,1)} %get-tuple-element.24), calls=%async_computation.2 | async-start | bytes 655360 | tf_op jit(solution)/shard_map/all_to_all | solution.py:469
  135.8 15.2 %copy-start.5 = (bf16[256,256]{1,0:T(8,128)(2,1)S(1)}, bf16[256,256]{1,0:T(8,128)(2,1)}, u32[]{:S(2)}) copy-start(bf16[256,256]{1,0:T(8,128)(2,1)} %ws.3) | copy-start | bytes 393220
  135.8 15.2 %copy-start.6 = (bf16[256,256]{1,0:T(8,128)(2,1)S(1)}, bf16[256,256]{1,0:T(8,128)(2,1)}, u32[]{:S(2)}) copy-start(bf16[256,256]{1,0:T(8,128)(2,1)} %wn.3) | copy-start | bytes 393220
  144.9 17.7 %all-to-all-start.3 = ((bf16[32,32,128]{2,1,0:T(8,128)(2,1)}), bf16[32,32,128]{2,1,0:T(8,128)(2,1)S(1)}, u32[]{:S(2)}, u32[]{:S(2)}) async-start(bf16[32,32,128]{2,1,0:T(8,128)(2,1)} %pad_maximum_fusion), calls=%async_computation.3 | async-start | bytes 524288 | tf_op jit(solution)/shard_map/all_to_all | solution.py:479
